TPU v7x, 256 devices: a whole 4x4x8 slice. The times are simulated.
256 devices in a mesh: dp: 32 (over z, y_hi, core), mp: 8 (over x, y_lo).
Axes of the slice: x: 4, y: 4 (y_hi: 2, y_lo: 2; y = y_hi * 2 + y_lo), z: 8, core: 2. Of those that a mesh axis runs over, the one named last changes fastest.
Arguments:
- token_ids: int32 [128, 64], P(None, 'dp'), may hold values from 0 to 1023
- fanout: int32 [128, 16], replicated, may hold values from 1 to 16
- table_of_column: int32 [64], P('dp'), may hold values from 0 to 15
- embed_table: bfloat16 [64, 1024, 1024], P('dp', 'mp'), may hold values from -35 to 35
- start_vector: bfloat16 [1024], replicated, may hold values from -6 to 6
- gain_attn: bfloat16 [1024], replicated, may hold values from 0.25 to 1.75
- gain_mlp: bfloat16 [1024], replicated, may hold values from 0.25 to 1.75
- gain_final: bfloat16 [1024], replicated, may hold values from 0.25 to 1.75
- w_qkv: bfloat16 [1024, 3, 1024], P(None, None, 'mp'), may hold values from -8 to 8
- w_out: bfloat16 [1024, 1024], P(None, 'mp'), may hold values from -0.1875 to 0.1875
- w_gate: bfloat16 [1024, 4096], P(None, 'mp'), may hold values from -0.1875 to 0.1875
- w_up: bfloat16 [1024, 4096], P(None, 'mp'), may hold values from -0.1875 to 0.1875
- w_down: bfloat16 [1024, 4096], P(None, 'mp'), may hold values from -0.09375 to 0.09375
Outputs:
- nll: float32 [128, 64], P(None, 'dp')
- grad_table: float32 [64, 1024, 1024], P('dp', 'mp')
- grad_qkv: float32 [1024, 3, 1024], P('dp', None, 'mp')
- grad_out: float32 [1024, 1024], P('dp', 'mp')
- grad_gate: float32 [1024, 4096], P('dp', 'mp')
- grad_up: float32 [1024, 4096], P('dp', 'mp')
- grad_down: float32 [1024, 4096], P('dp', 'mp')
All inputs are finite; a program needn't handle non-finite values.
Results may differ from a plain program's by a relative error of at most 0.015.
The roundings to bfloat16 on the way count: a program that leaves them out, or rounds other values in their place, can miss the bound.
Values may be sent and summed in bfloat16 or wider, within the bound.
A program may use at most 128 MiB of HBM per device.

v0:
```python
import math

import jax
import jax.numpy as jnp
from jax import lax
from jax.sharding import PartitionSpec as P

HS = 64
TABLES = 16


EPS = 1e-05
ATTN_CAP = 50.0
LOGIT_CAP = 30.0


def gather_features(values):
    return lax.all_gather(values, "mp", axis=2, tiled=True)


def feature_sum(term):
    return lax.psum_scatter(term, "mp", scatter_dimension=2, tiled=True)


def cols_to_rows(values):
    return lax.all_to_all(values, "dp", split_axis=0, concat_axis=1, tiled=True)


def rows_to_cols(values):
    return lax.all_to_all(values, "dp", split_axis=1, concat_axis=0, tiled=True)


def rms_of(values):
    floats = values.astype(jnp.float32)
    return jnp.sqrt(jnp.mean(floats * floats, axis=-1, keepdims=True) + EPS)


def normalize(values, gain, rms):
    return (values.astype(jnp.float32) / rms * gain.astype(jnp.float32)).astype(jnp.bfloat16)


def norm_back_full(values, d_norm, gain, rms):
    floats = values.astype(jnp.float32)
    gains = gain.astype(jnp.float32)
    total = jnp.sum(gains * d_norm * floats, axis=-1, keepdims=True)
    return gains * d_norm / rms - floats * total / (floats.shape[-1] * rms * rms * rms)


def norm_back_part(values, d_norm, gain, rms, model_width):
    floats = values.astype(jnp.float32)
    gains = gain.astype(jnp.float32)
    partial_total = jnp.sum(gains * d_norm * floats, axis=-1)
    total = lax.psum(partial_total, "mp")[..., None]
    return gains * d_norm / rms - floats * total / (model_width * rms * rms * rms)


def local(
    token_ids,
    fanout,
    table_of_column,
    embed_table,
    start_vector,
    gain_attn,
    gain_mlp,
    gain_final,
    w_qkv,
    w_out,
    w_gate,
    w_up,
    w_down,
):
    fl = jnp.float32
    mp_rank = lax.axis_index("mp")
    mp_count = lax.axis_size("mp")
    model_width = embed_table.shape[2]
    vocab_part = embed_table.shape[1]
    part_width = model_width // mp_count
    head_cols = w_qkv.shape[2]
    local_heads = head_cols // HS
    row_total_count = token_ids.shape[0]

    def own_part(vector):
        return lax.dynamic_slice_in_dim(vector, mp_rank * part_width, part_width, 0)

    local_ids = token_ids - mp_rank * vocab_part
    onehot = (
        local_ids[:, :, None] == jnp.arange(vocab_part, dtype=jnp.int32)[None, None, :]
    ).astype(jnp.bfloat16)
    picked = jnp.einsum("rcv,cvd->rcd", onehot, embed_table, preferred_element_type=fl)
    emb_cols = feature_sum(picked).astype(jnp.bfloat16)
    emb_rows = cols_to_rows(emb_cols)
    rows_here = emb_rows.shape[0]
    col_count = emb_rows.shape[1]
    start_rows = jnp.broadcast_to(own_part(start_vector)[None, None, :], (rows_here, 1, part_width))
    resid_in = jnp.concatenate([start_rows, emb_rows[:, :-1]], axis=1)
    in_full = gather_features(resid_in)
    rms_attn = rms_of(in_full)
    norm_attn = normalize(in_full, gain_attn, rms_attn)
    qkv = jnp.einsum("rpd,dtx->rptx", norm_attn, w_qkv, preferred_element_type=fl).astype(
        jnp.bfloat16
    )
    queries = qkv[:, :, 0].reshape(rows_here, col_count, local_heads, HS)
    key_rows = qkv[:, :, 1].reshape(rows_here, col_count, local_heads, HS)
    value_rows = qkv[:, :, 2].reshape(rows_here, col_count, local_heads, HS)
    score_raw = jnp.einsum(
        "rqhe,rkhe->rhqk", queries, key_rows, preferred_element_type=fl
    ) / math.sqrt(HS)
    score = ATTN_CAP * jnp.tanh(score_raw / ATTN_CAP)
    col_index = jnp.arange(col_count, dtype=jnp.int32)
    causal = col_index[:, None] >= col_index[None, :]
    exp_score = jnp.where(causal, jnp.exp(score), 0.0)
    attn_prob = exp_score / jnp.sum(exp_score, axis=-1, keepdims=True)
    prob_b = attn_prob.astype(jnp.bfloat16)
    attn_heads = jnp.einsum(
        "rhqk,rkhe->rqhe", prob_b, value_rows, preferred_element_type=fl
    ).astype(jnp.bfloat16)
    attn_out = attn_heads.reshape(rows_here, col_count, head_cols)
    mixed_part = jnp.einsum("rpj,dj->rpd", attn_out, w_out, preferred_element_type=fl)
    resid_mid = (resid_in.astype(fl) + feature_sum(mixed_part)).astype(jnp.bfloat16)
    mid_full = gather_features(resid_mid)
    rms_mlp = rms_of(mid_full)
    norm_mlp = normalize(mid_full, gain_mlp, rms_mlp)
    gate_pre = jnp.einsum("rpd,df->rpf", norm_mlp, w_gate, preferred_element_type=fl)
    up_proj = jnp.einsum("rpd,df->rpf", norm_mlp, w_up, preferred_element_type=fl)
    hidden = (jax.nn.silu(gate_pre) * up_proj).astype(jnp.bfloat16)
    down_part = jnp.einsum("rpf,df->rpd", hidden, w_down, preferred_element_type=fl)
    resid_out = (resid_mid.astype(fl) + feature_sum(down_part)).astype(jnp.bfloat16)
    out_cols = rows_to_cols(resid_out)
    out_full = gather_features(out_cols)
    rms_final = rms_of(out_full)
    norm_final = normalize(out_full, gain_final, rms_final)
    width_root = math.sqrt(model_width)
    logit_raw = (
        jnp.einsum("rcd,cvd->rcv", norm_final, embed_table, preferred_element_type=fl) / width_root
    )
    capped = LOGIT_CAP * jnp.tanh(logit_raw / LOGIT_CAP)
    exp_logit = jnp.exp(capped)
    onehot_f = onehot.astype(fl)
    exp_total, target_logit = lax.psum(
        (jnp.sum(exp_logit, axis=-1), jnp.sum(capped * onehot_f, axis=-1)), "mp"
    )
    nll = jnp.log(exp_total) - target_logit
    select = table_of_column[None, :, None] == jnp.arange(TABLES, dtype=jnp.int32)[None, None, :]
    counts = jnp.sum(jnp.where(select, fanout[:, None, :], 0), axis=-1).astype(fl)
    row_scale = 1.0 / (counts * row_total_count)
    ratio = capped / LOGIT_CAP
    d_logit = (
        (exp_logit / exp_total[:, :, None] - onehot_f)
        * row_scale[:, :, None]
        * (1.0 - ratio * ratio)
    ).astype(jnp.bfloat16)
    d_final_part = (
        jnp.einsum("rcv,cvd->rcd", d_logit, embed_table, preferred_element_type=fl) / width_root
    )
    table_grad = (
        jnp.einsum("rcv,rcd->cvd", d_logit, norm_final, preferred_element_type=fl) / width_root
    )
    d_final = lax.psum(d_final_part, "mp")
    back_full = norm_back_full(out_full, d_final, gain_final, rms_final)
    d_out_cols = lax.dynamic_slice_in_dim(back_full, mp_rank * part_width, part_width, 2).astype(
        jnp.bfloat16
    )
    d_out = cols_to_rows(d_out_cols)
    d_out_full = gather_features(d_out)
    d_hidden = jnp.einsum("rpd,df->rpf", d_out_full, w_down, preferred_element_type=fl)
    sigmoid_gate = jax.nn.sigmoid(gate_pre)
    d_gate = (d_hidden * up_proj * sigmoid_gate * (1.0 + gate_pre * (1.0 - sigmoid_gate))).astype(
        jnp.bfloat16
    )
    d_up = (d_hidden * gate_pre * sigmoid_gate).astype(jnp.bfloat16)
    d_norm_mlp = jnp.einsum("rpf,df->rpd", d_gate, w_gate, preferred_element_type=fl) + jnp.einsum(
        "rpf,df->rpd", d_up, w_up, preferred_element_type=fl
    )
    d_mid = (
        d_out.astype(fl)
        + norm_back_part(
            resid_mid, feature_sum(d_norm_mlp), own_part(gain_mlp), rms_mlp, model_width
        )
    ).astype(jnp.bfloat16)
    mid_grad_full = gather_features(d_mid)
    d_attn = jnp.einsum("rpd,dj->rpj", mid_grad_full, w_out, preferred_element_type=fl).astype(
        jnp.bfloat16
    )
    d_attn = d_attn.reshape(rows_here, col_count, local_heads, HS)
    d_prob = jnp.einsum("rqhe,rkhe->rhqk", d_attn, value_rows, preferred_element_type=fl)
    ratio_s = score / ATTN_CAP
    d_score = attn_prob * (d_prob - jnp.sum(attn_prob * d_prob, axis=-1, keepdims=True))
    d_scaled = (d_score * (1.0 - ratio_s * ratio_s) / math.sqrt(HS)).astype(jnp.bfloat16)
    d_query = jnp.einsum("rhqk,rkhe->rqhe", d_scaled, key_rows, preferred_element_type=fl)
    d_key = jnp.einsum("rhqk,rqhe->rkhe", d_scaled, queries, preferred_element_type=fl)
    d_value = jnp.einsum("rhqk,rqhe->rkhe", prob_b, d_attn, preferred_element_type=fl)
    d_qkv = (
        jnp.stack([d_query, d_key, d_value], axis=2)
        .reshape(rows_here, col_count, 3, head_cols)
        .astype(jnp.bfloat16)
    )
    d_norm_attn = jnp.einsum("rptx,dtx->rpd", d_qkv, w_qkv, preferred_element_type=fl)
    d_in = (
        d_mid.astype(fl)
        + norm_back_part(
            resid_in, feature_sum(d_norm_attn), own_part(gain_attn), rms_attn, model_width
        )
    ).astype(jnp.bfloat16)
    d_embed_rows = jnp.concatenate(
        [d_in[:, 1:], jnp.zeros((rows_here, 1, part_width), jnp.bfloat16)], axis=1
    )
    d_embed_cols = rows_to_cols(d_embed_rows)
    d_embed_full = gather_features(d_embed_cols)
    table_grad = table_grad + jnp.einsum(
        "rcv,rcd->cvd", onehot, d_embed_full, preferred_element_type=fl
    )
    qkv_term = jnp.einsum("rpd,rptx->dtx", norm_attn, d_qkv, preferred_element_type=fl).reshape(
        model_width, 3 * head_cols
    )
    out_term = jnp.einsum("rpd,rpj->dj", mid_grad_full, attn_out, preferred_element_type=fl)
    whole_terms = jnp.concatenate(
        [
            jnp.concatenate([qkv_term, out_term], axis=1),
            jnp.concatenate(
                [
                    jnp.einsum("rpd,rpf->df", norm_mlp, d_gate, preferred_element_type=fl),
                    jnp.einsum("rpd,rpf->df", norm_mlp, d_up, preferred_element_type=fl),
                    jnp.einsum("rpd,rpf->df", d_out_full, hidden, preferred_element_type=fl),
                ],
                axis=1,
            ),
        ],
        axis=1,
    )
    summed = lax.psum_scatter(whole_terms, "dp", scatter_dimension=0, tiled=True)
    ff_part = w_gate.shape[1]
    qkv_width = 3 * head_cols
    grad_qkv = summed[:, :qkv_width].reshape(summed.shape[0], 3, head_cols)
    grad_out = summed[:, qkv_width : qkv_width + head_cols]
    base = qkv_width + head_cols
    grad_gate = summed[:, base : base + ff_part]
    grad_up = summed[:, base + ff_part : base + 2 * ff_part]
    grad_down = summed[:, base + 2 * ff_part : base + 3 * ff_part]
    return (nll, table_grad, grad_qkv, grad_out, grad_gate, grad_up, grad_down)


def solution(mesh):
    return jax.shard_map(
        local,
        mesh=mesh,
        in_specs=(
            P(None, "dp"),
            P(),
            P("dp"),
            P("dp", "mp", None),
            P(),
            P(),
            P(),
            P(),
            P(None, None, "mp"),
            P(None, "mp"),
            P(None, "mp"),
            P(None, "mp"),
            P(None, "mp"),
        ),
        out_specs=(
            P(None, "dp"),
            P("dp", "mp", None),
            P("dp", None, "mp"),
            P("dp", "mp"),
            P("dp", "mp"),
            P("dp", "mp"),
            P("dp", "mp"),
        ),
        check_vma=False,
    )
```

profile of v0, /device:TPU:2, one launch (start us, length us, event | category | flops | bytes accessed | tf_op | source)
XLA Modules:
  0.0 726.3 jit_solution(7134462608592402723)
XLA Ops:
  10.4 44.1 %reduce-scatter.9.cloned.1.call-done = f32[128,2,128]{2,0,1:T(8,128)} async-done(((f32[128,2,1024]{2,0,1:T(8,128)}), f32[128,2,128]{2,0,1:T(8,128)}) %reduce-scatter.9.cloned.1.call-update) | async-done | bytes 131088 | tf_op jit(solution)/shard_map/reduce_scatter | solution.py:22
  56.1 10.0 %all-to-all-start = ((bf16[128,2,128]{2,1,0:T(2,128)(2,1)}), bf16[128,2,128]{2,1,0:T(2,128)(2,1)S(1)}, u32[]{:S(2)}, u32[]{:S(2)}) async-start(bf16[128,2,128]{2,1,0:T(2,128)(2,1)} %copy.114), calls=%async_computation.1 | async-start | bytes 131072 | tf_op jit(solution)/shard_map/all_to_all | solution.py:26
  67.7 8.4 %all-to-all-done = bf16[128,2,128]{2,1,0:T(2,128)(2,1)S(1)} async-done(((bf16[128,2,128]{2,1,0:T(2,128)(2,1)}), bf16[128,2,128]{2,1,0:T(2,128)(2,1)S(1)}, u32[]{:S(2)}, u32[]{:S(2)}) %all-to-all-start) | async-done | bytes 65568 | tf_op jit(solution)/shard_map/all_to_all | solution.py:26
  76.8 26.7 %all_gather.18 = bf16[4,64,1024]{2,1,0:T(8,128)(2,1)S(1)} all-gather(bf16[4,64,128]{2,1,0:T(8,128)(2,1)S(1)} %get-tuple-element.52), channel_id=1, replica_groups=mesh['dp'=32,'mp'=8] {'mp'}, dimensions={2}, use_global_device_ids=true | all-gather | bytes 589824 | tf_op jit(solution)/shard_map/all_gather | solution.py:18
  108.4 34.5 %reduce-scatter.11.cloned.1.call-done = f32[4,64,128]{2,1,0:T(8,128)} async-done(((f32[4,64,1024]{2,1,0:T(8,128)}), f32[4,64,128]{2,1,0:T(8,128)}) %reduce-scatter.11.cloned.1.call-update) | async-done | bytes 131088 | tf_op jit(solution)/shard_map/reduce_scatter | solution.py:22
  143.8 26.9 %all_gather.19 = bf16[4,64,1024]{2,1,0:T(8,128)(2,1)S(1)} all-gather(bf16[4,64,128]{2,1,0:T(8,128)(2,1)S(1)} %add_convert_fusion), channel_id=1, replica_groups=mesh['dp'=32,'mp'=8] {'mp'}, dimensions={2}, use_global_device_ids=true | all-gather | bytes 589824 | tf_op jit(solution)/shard_map/all_gather | solution.py:18
  178.3 40.9 %reduce-scatter.13.cloned.1.call-done = f32[4,64,128]{2,1,0:T(8,128)} async-done(((f32[4,64,1024]{2,1,0:T(8,128)}), f32[4,64,128]{2,1,0:T(8,128)}) %reduce-scatter.13.cloned.1.call-update) | async-done | bytes 131088 | tf_op jit(solution)/shard_map/reduce_scatter | solution.py:22
  220.9 10.0 %all-to-all-start.1 = ((bf16[4,64,128]{2,0,1:T(4,128)(2,1)}), bf16[4,64,128]{2,0,1:T(4,128)(2,1)S(1)}, u32[]{:S(2)}, u32[]{:S(2)}) async-start(bf16[4,64,128]{2,0,1:T(4,128)(2,1)} %copy.121), calls=%async_computation.4 | async-start | bytes 131072 | tf_op jit(solution)/shard_map/all_to_all | solution.py:30
  231.5 9.3 %all-to-all-done.1 = bf16[4,64,128]{2,0,1:T(4,128)(2,1)S(1)} async-done(((bf16[4,64,128]{2,0,1:T(4,128)(2,1)}), bf16[4,64,128]{2,0,1:T(4,128)(2,1)S(1)}, u32[]{:S(2)}, u32[]{:S(2)}) %all-to-all-start.1) | async-done | bytes 65568 | tf_op jit(solution)/shard_map/all_to_all | solution.py:30
  240.9 26.7 %all_gather.20 = bf16[128,2,1024]{2,0,1:T(8,128)(2,1)S(1)} all-gather(bf16[128,2,128]{2,0,1:T(8,128)(2,1)S(1)} %bitcast.144), channel_id=1, replica_groups=mesh['dp'=32,'mp'=8] {'mp'}, dimensions={2}, use_global_device_ids=true | all-gather | bytes 589824 | tf_op jit(solution)/shard_map/all_gather | solution.py:18
  269.9 14.4 %psum.35 = f32[128,2]{0,1:T(2,128)S(1)} all-reduce(f32[128,2]{0,1:T(2,128)} %get-tuple-element.35), channel_id=1, replica_groups=mesh['dp'=32,'mp'=8] {'mp'}, use_global_device_ids=true, to_apply=%region_8.9 | all-reduce | flops 256 | bytes 2048 | tf_op jit(solution)/shard_map/psum | solution.py:139
  287.8 76.1 %all-reduce.4.cloned.1.call-done = f32[128,2,1024]{2,0,1:T(8,128)} async-done(((f32[128,2,1024]{2,0,1:T(8,128)}), f32[128,2,1024]{2,0,1:T(8,128)}) %all-reduce.4.cloned.1.call-update) | async-done | bytes 1048592 | tf_op jit(solution)/shard_map/psum | solution.py:158
  366.6 19.4 %all_to_all.72 = bf16[128,2,128]{2,1,0:T(2,128)(2,1)S(1)} all-to-all(bf16[128,2,128]{2,1,0:T(2,128)(2,1)S(1)} %copy.124), channel_id=1, replica_groups=mesh['dp'=32,'mp'=8] {'dp'}, dimensions={0} | all-to-all | bytes 131072 | tf_op jit(solution)/shard_map/all_to_all | solution.py:26
  386.1 26.0 %all_gather.21 = bf16[4,64,1024]{2,1,0:T(8,128)(2,1)S(1)} all-gather(bf16[4,64,128]{2,1,0:T(8,128)(2,1)S(1)} %bitcast.138), channel_id=1, replica_groups=mesh['dp'=32,'mp'=8] {'mp'}, dimensions={2}, use_global_device_ids=true | all-gather | bytes 589824 | tf_op jit(solution)/shard_map/all_gather | solution.py:18
  417.6 33.3 %reduce-scatter.15.cloned.1.call-done = f32[4,64,128]{2,1,0:T(8,128)} async-done(((f32[4,64,1024]{2,1,0:T(8,128)}), f32[4,64,128]{2,1,0:T(8,128)}) %reduce-scatter.15.cloned.1.call-update) | async-done | bytes 131088 | tf_op jit(solution)/shard_map/reduce_scatter | solution.py:22
  452.5 18.0 %psum.38 = f32[4,64]{1,0:T(4,128)} all-reduce(f32[4,64]{1,0:T(4,128)} %fusion.46), channel_id=1, replica_groups=mesh['dp'=32,'mp'=8] {'mp'}, use_global_device_ids=true, to_apply=%region_16.17 | all-reduce | flops 256 | bytes 2048 | tf_op jit(solution)/shard_map/psum | solution.py:53
  472.2 27.0 %all_gather.22 = bf16[4,64,1024]{2,1,0:T(8,128)(2,1)S(1)} all-gather(bf16[4,64,128]{2,1,0:T(8,128)(2,1)S(1)} %fusion.61), channel_id=1, replica_groups=mesh['dp'=32,'mp'=8] {'mp'}, dimensions={2}, use_global_device_ids=true | all-gather | bytes 589824 | tf_op jit(solution)/shard_map/all_gather | solution.py:18
  525.4 9.2 %copy.156 = f32[1024,2048]{1,0:T(8,128)} copy(f32[1024,2048]{0,1:T(8,128)} %bitcast_dynamic-update-slice_fusion) | data formatting | bytes 16777216
  537.2 17.6 %reduce-scatter.17.cloned.1.call-done = f32[4,64,128]{2,1,0:T(8,128)} async-done(((f32[4,64,1024]{2,1,0:T(8,128)}), f32[4,64,128]{2,1,0:T(8,128)}) %reduce-scatter.17.cloned.1.call-update) | async-done | bytes 131088 | tf_op jit(solution)/shard_map/reduce_scatter | solution.py:22
  555.9 17.3 %all-reduce.1 = (f32[128,2]{0,1:T(2,128)S(1)}, f32[4,64]{1,0:T(4,128)S(1)}) all-reduce(f32[128,2]{0,1:T(2,128)S(1)} %copy-done.36, f32[4,64]{1,0:T(4,128)S(1)} %get-tuple-element.39), channel_id=1, replica_groups=mesh['dp'=32,'mp'=8] {'mp'}, use_global_device_ids=true, to_apply=%region_10.11 | all-reduce | flops 512 | bytes 4096 | tf_op jit(solution)/shard_map/psum | solution.py:139
  574.1 10.0 %all-to-all-start.3 = ((bf16[4,64,128]{2,0,1:T(4,128)(2,1)}), bf16[4,64,128]{2,0,1:T(4,128)(2,1)S(1)}, u32[]{:S(2)}, u32[]{:S(2)}) async-start(bf16[4,64,128]{2,0,1:T(4,128)(2,1)} %concatenate.12.clone), calls=%async_computation.8 | async-start | bytes 131072 | tf_op jit(solution)/shard_map/all_to_all | solution.py:30
  584.6 9.4 %all-to-all-done.3 = bf16[4,64,128]{2,0,1:T(4,128)(2,1)S(1)} async-done(((bf16[4,64,128]{2,0,1:T(4,128)(2,1)}), bf16[4,64,128]{2,0,1:T(4,128)(2,1)S(1)}, u32[]{:S(2)}, u32[]{:S(2)}) %all-to-all-start.3) | async-done | bytes 65568 | tf_op jit(solution)/shard_map/all_to_all | solution.py:30
  594.0 28.0 %all_gather.23 = bf16[128,2,1024]{2,0,1:T(8,128)(2,1)S(1)} all-gather(bf16[128,2,128]{2,0,1:T(8,128)(2,1)S(1)} %bitcast.145), channel_id=1, replica_groups=mesh['dp'=32,'mp'=8] {'mp'}, dimensions={2}, use_global_device_ids=true | all-gather | bytes 589824 | tf_op jit(solution)/shard_map/all_gather | solution.py:18
  624.5 90.4 %reduce-scatter.19.cloned.1.call-done = f32[32,2048]{1,0:T(8,128)} async-done(((f32[1024,2048]{1,0:T(8,128)}), f32[32,2048]{1,0:T(8,128)}) %reduce-scatter.19.cloned.1.call-update) | async-done | bytes 262160
  (177 shorter events, 78.1 us)
Async XLA Ops:
  7.2 169.5 %copy-start = (bf16[1024,512]{1,0:T(8,128)(2,1)S(1)}, bf16[1024,512]{1,0:T(8,128)(2,1)}, u32[]{:S(2)}) copy-start(bf16[1024,512]{1,0:T(8,128)(2,1)} %param.25) | copy-start | bytes 3145732
  7.2 99.8 %copy-start.6 = (bf16[1024,128]{1,0:T(8,128)(2,1)S(1)}, bf16[1024,128]{1,0:T(8,128)(2,1)}, u32[]{:S(2)}) copy-start(bf16[1024,128]{1,0:T(8,128)(2,1)} %param.22) | copy-start | bytes 786436
  7.2 101.1 %copy-start.35 = (bf16[1024]{0:T(1024)(128)(2,1)S(1)}, bf16[1024]{0:T(1024)(128)(2,1)}, u32[]{:S(2)}) copy-start(bf16[1024]{0:T(1024)(128)(2,1)} %param.19) | copy-start | bytes 6148
  7.2 47.3 %reduce-scatter.9.cloned.1.call-start = ((), (), s32[]{:S(2)}) async-start(), calls=%async_computation.10 | async-start | bytes 1179648 | tf_op jit(solution)/shard_map/reduce_scatter | solution.py:22
  56.1 20.0 %all-to-all-start = ((bf16[128,2,128]{2,1,0:T(2,128)(2,1)}), bf16[128,2,128]{2,1,0:T(2,128)(2,1)S(1)}, u32[]{:S(2)}, u32[]{:S(2)}) async-start(bf16[128,2,128]{2,1,0:T(2,128)(2,1)} %copy.114), calls=%async_computation.1 | async-start | bytes 131072 | tf_op jit(solution)/shard_map/all_to_all | solution.py:26
  66.1 76.7 %reduce-scatter.11.cloned.1.call-start = ((), (), s32[]{:S(2)}) async-start(), calls=%async_computation.11 | async-start | bytes 1179648 | tf_op jit(solution)/shard_map/reduce_scatter | solution.py:22
  66.9 39.3 %copy-start.30 = (f32[1024]{0:T(1024)}, f32[1024]{0:T(1024)S(1)}, u32[]{:S(2)}) copy-start(f32[1024]{0:T(1024)S(1)} %convert_element_type.117) | copy-start | bytes 12292
  67.7 76.2 %copy-start.28 = (pred[64,64]{0,1:T(8,128)(4,1)}, pred[64,64]{0,1:T(8,128)(4,1)S(1)}, u32[]{:S(2)}) copy-start(pred[64,64]{0,1:T(8,128)(4,1)S(1)} %iota_compare_fusion.3) | copy-start | bytes 12292
  106.7 64.0 %copy-start.39 = (f32[4,2,64]{2,1,0:T(2,128)}, f32[4,2,64]{2,1,0:T(2,128)S(1)}, u32[]{:S(2)}) copy-start(f32[4,2,64]{2,1,0:T(2,128)S(1)} %get-tuple-element.59) | copy-start | bytes 6148
  108.3 111.0 %reduce-scatter.13.cloned.1.call-start = ((), (), s32[]{:S(2)}) async-start(), calls=%async_computation.12 | async-start | bytes 1179648 | tf_op jit(solution)/shard_map/reduce_scatter | solution.py:22
  108.4 69.7 %copy-start.31 = (f32[1024]{0:T(1024)}, f32[1024]{0:T(1024)S(1)}, u32[]{:S(2)}) copy-start(f32[1024]{0:T(1024)S(1)} %convert_element_type.126) | copy-start | bytes 12292
  171.5 96.8 %copy-start.1 = (bf16[2,128,1024]{2,1,0:T(8,128)(2,1)S(1)}, bf16[2,128,1024]{2,1,0:T(8,128)(2,1)}, u32[]{:S(2)}) copy-start(bf16[2,128,1024]{2,1,0:T(8,128)(2,1)} %param.16) | copy-start | bytes 1572868
  176.7 64.2 %copy-start.7 = (bf16[4,64,512]{2,1,0:T(8,128)(2,1)}, bf16[4,64,512]{2,1,0:T(8,128)(2,1)S(1)}, u32[]{:S(2)}) copy-start(bf16[4,64,512]{2,1,0:T(8,128)(2,1)S(1)} %get-tuple-element.61) | copy-start | bytes 786436
  220.9 20.0 %all-to-all-start.1 = ((bf16[4,64,128]{2,0,1:T(4,128)(2,1)}), bf16[4,64,128]{2,0,1:T(4,128)(2,1)S(1)}, u32[]{:S(2)}, u32[]{:S(2)}) async-start(bf16[4,64,128]{2,0,1:T(4,128)(2,1)} %copy.121), calls=%async_computation.4 | async-start | bytes 131072 | tf_op jit(solution)/shard_map/all_to_all | solution.py:30
  230.9 133.0 %all-reduce.4.cloned.1.call-start = ((), (), s32[]{:S(2)}) async-start(), calls=%async_computation.13 | async-start | bytes 2097152 | tf_op jit(solution)/shard_map/psum | solution.py:158
  286.6 164.3 %reduce-scatter.15.cloned.1.call-start = ((), (), s32[]{:S(2)}) async-start(), calls=%async_computation.14 | async-start | bytes 1179648 | tf_op jit(solution)/shard_map/reduce_scatter | solution.py:22
  363.9 50.2 %copy-start.4 = (bf16[1024,512]{1,0:T(8,128)(2,1)S(1)}, bf16[1024,512]{1,0:T(8,128)(2,1)}, u32[]{:S(2)}) copy-start(bf16[1024,512]{1,0:T(8,128)(2,1)} %param.23) | copy-start | bytes 3145732
  363.9 51.0 %copy-start.5 = (bf16[1024,512]{1,0:T(8,128)(2,1)S(1)}, bf16[1024,512]{1,0:T(8,128)(2,1)}, u32[]{:S(2)}) copy-start(bf16[1024,512]{1,0:T(8,128)(2,1)} %param.24) | copy-start | bytes 3145732
  412.1 58.4 %copy-start.2 = (bf16[4,64,1024]{2,1,0:T(8,128)(2,1)}, bf16[4,64,1024]{2,1,0:T(8,128)(2,1)S(1)}, u32[]{:S(2)}) copy-start(bf16[4,64,1024]{2,1,0:T(8,128)(2,1)S(1)} %all_gather.21) | copy-start | bytes 1572868
  416.3 138.5 %reduce-scatter.17.cloned.1.call-start = ((), (), s32[]{:S(2)}) async-start(), calls=%async_computation.15 | async-start | bytes 1179648 | tf_op jit(solution)/shard_map/reduce_scatter | solution.py:22
  513.3 201.6 %reduce-scatter.19.cloned.1.call-start = ((), (), s32[]{:S(2)}) async-start(), calls=%async_computation.16 | async-start | bytes 8650752
  534.7 38.5 %copy-start.10 = (bf16[4,64,128]{2,1,0:T(8,128)(2,1)S(1)}, bf16[4,64,128]{2,1,0:T(8,128)(2,1)}, u32[]{:S(2)}) copy-start(bf16[4,64,128]{2,1,0:T(8,128)(2,1)} %copy-done.9) | copy-start | bytes 196612
  534.7 38.5 %copy-start.12 = (f32[4,64,128]{2,1,0:T(8,128)S(1)}, f32[4,64,128]{2,1,0:T(8,128)}, u32[]{:S(2)}) copy-start(f32[4,64,128]{2,1,0:T(8,128)} %get-tuple-element.51) | copy-start | bytes 393220
  574.1 19.9 %all-to-all-start.3 = ((bf16[4,64,128]{2,0,1:T(4,128)(2,1)}), bf16[4,64,128]{2,0,1:T(4,128)(2,1)S(1)}, u32[]{:S(2)}, u32[]{:S(2)}) async-start(bf16[4,64,128]{2,0,1:T(4,128)(2,1)} %concatenate.12.clone), calls=%async_computation.8 | async-start | bytes 131072 | tf_op jit(solution)/shard_map/all_to_all | solution.py:30
  (27 other events, 268.3 us)
Sparse Core Ops, SparseCore 0:
  11.1 43.3 reduce-scatter.8
  108.4 34.4 reduce-scatter.10
  178.3 40.9 reduce-scatter.12
  286.7 77.0 all-reduce.3
  416.4 34.4 reduce-scatter.14
  513.4 41.3 reduce-scatter.16
  559.2 155.6 reduce-scatter.18
where the time goes:
time: 728 us; the launch traced here: 726 us
  waiting for transfers between devices  364 us (50%)
  blocking collectives  230 us (32%)
  matrix products  46 us (6%)
  starting transfers between devices  30.4 us (4%)
  local copies, waits for them, and re-layouts  22.4 us (3%)
  other arithmetic  18.3 us (3%)
  between operations  14.7 us (2%)
    reduce_scatter x5, waiting for transfers between devices, feature_sum(): return lax.psum_scatter(term, 'mp', scatter_dimension=2, tiled=True)  170 us
    all_gather x6, blocking collectives, gather_features(): return lax.all_gather(values, 'mp', axis=2, tiled=True)  161 us
    unnamed x8, waiting for transfers between devices  90.5 us
    psum x1, waiting for transfers between devices, local(): d_final = lax.psum(d_final_part, 'mp')  76.1 us
    psum x2, blocking collectives, local(): lax.psum((jnp.sum(exp_logit, axis=-1), jnp.sum(capped * onehot_f, axis=-1...  31.7 us
    all_to_all x2, starting transfers between devices, rows_to_cols(): return lax.all_to_all(values, 'dp', split_axis=1, concat_axis=0, tiled=True)  20 us
    all_to_all x1, blocking collectives, cols_to_rows(): return lax.all_to_all(values, 'dp', split_axis=0, concat_axis=1, tiled=True)  19.4 us
    all_to_all x2, waiting for transfers between devices, rows_to_cols(): return lax.all_to_all(values, 'dp', split_axis=1, concat_axis=0, tiled=True)  18.7 us
  transfers between devices with their start and end apart: 10, of which 10 were waited for; matrix products, arithmetic and copies ran while one was open for 5% of the time, Pallas kernels for 0%

commit v1 on v0

v1 whole, which is shorter than its diff:
```python
import functools
import math

import jax
import jax.numpy as jnp
from jax import lax
from jax.experimental import pallas as pl
from jax.experimental.pallas import tpu as pltpu
from jax.sharding import PartitionSpec as P

HS = 64
TABLES = 16
EPS = 1e-05
ATTN_CAP = 50.0
LOGIT_CAP = 30.0
MESH = pl.DeviceIdType.MESH
FL = jnp.float32
BF = jnp.bfloat16
LANES = 128


def rms_of(floats):
    return jnp.sqrt(jnp.mean(floats * floats, axis=-1, keepdims=True) + EPS)


def norm_back(floats, d_norm, gains):
    rms = rms_of(floats)
    total = jnp.sum(gains * d_norm * floats, axis=-1, keepdims=True)
    return gains * d_norm / rms - floats * total / (floats.shape[-1] * rms * rms * rms)


def enter(n_dp, n_mp, me_dp, me_mp, exchange):
    barrier = pltpu.get_barrier_semaphore()

    def greet(axis, me, count):
        def one(off, carry):
            pl.semaphore_signal(
                barrier, inc=1, device_id={axis: lax.rem(me + off, count)}, device_id_type=MESH
            )
            return carry

        lax.fori_loop(1, count, one, 0)

    greet("mp", me_mp, n_mp)
    if exchange:
        greet("dp", me_dp, n_dp)
    pl.semaphore_wait(barrier, n_mp - 1 + (n_dp - 1 if exchange else 0))


def scatter_sum(partial, landed, send, recv, me, n, slot_of):
    size = partial.shape[0] // n
    copies = []
    for off in range(1, n):
        peer = lax.rem(me + off, n)
        copy = pltpu.make_async_remote_copy(
            src_ref=partial.at[pl.ds(pl.multiple_of(slot_of(peer) * size, size), size)],
            dst_ref=landed.at[off],
            send_sem=send.at[off],
            recv_sem=recv.at[off],
            device_id={"mp": peer},
            device_id_type=MESH,
        )
        copy.start()
        copies.append(copy)
    total = partial[pl.ds(pl.multiple_of(slot_of(me) * size, size), size), :].astype(FL)
    for off, copy in enumerate(copies, 1):
        copy.wait_recv()
        total = total + landed[off].astype(FL)
    for copy in copies:
        copy.wait_send()
    return total


def gather_slots(shard, full, send, recv, me, n, slot):
    size = shard.shape[0]
    where = pl.ds(pl.multiple_of(slot * size, size), size)
    copies = []
    for off in range(1, n):
        copy = pltpu.make_async_remote_copy(
            src_ref=shard,
            dst_ref=full.at[where],
            send_sem=send.at[off],
            recv_sem=recv.at[off],
            device_id={"mp": lax.rem(me + off, n)},
            device_id_type=MESH,
        )
        copy.start()
        copies.append(copy)
    full[where, :] = shard[...]
    for copy in copies:
        copy.wait()


def swap_tokens(values, wide, outgo, income, send, recv, me, n, shift_out, shift_in):
    count, width = values.shape
    parts = width // LANES
    for part in range(parts):
        wide[pl.ds(part, count, stride=parts), :] = values[:, part * LANES : (part + 1) * LANES]
    outgo[...] = wide[...].reshape(count, parts, LANES).astype(BF)
    spot = lax.rem(me + shift_in, n)

    def copy_of(off):
        peer = lax.rem(me + off, n)
        return pltpu.make_async_remote_copy(
            src_ref=outgo.at[lax.rem(peer + shift_out, n)],
            dst_ref=income.at[spot],
            send_sem=send.at[off],
            recv_sem=recv.at[off],
            device_id={"dp": peer},
            device_id_type=MESH,
        )

    def start(off, carry):
        copy_of(off).start()
        return carry

    def finish(off, carry):
        copy_of(off).wait()
        return carry

    lax.fori_loop(1, n, start, 0)
    income[spot] = outgo[lax.rem(me + shift_out, n)]
    lax.fori_loop(1, n, finish, 0)
    wide[...] = income[...].astype(FL).reshape(count * parts, LANES)
    return jnp.concatenate(
        [wide[pl.ds(part, count, stride=parts), :] for part in range(parts)], axis=1
    )


def flipped(slot):
    return slot + 1 - 2 * lax.rem(slot, 2)


def same(slot):
    return slot


def own_rows(ref, slot, size):
    return ref[pl.ds(pl.multiple_of(slot * size, size), size), :].astype(FL)


def step_kernel(kind, n_dp, n_mp, *refs):
    exchange = kind in ("embed", "to_cols", "to_rows", "d_embed")
    n_in = {"embed": 2, "mid": 2, "to_cols": 2, "to_rows": 3, "d_mid": 4, "d_embed": 4}[kind]
    ins, full, scratch = refs[:n_in], refs[n_in], refs[n_in + 1 :]
    landed, shard, rs_send, rs_recv, ag_send, ag_recv = scratch[:6]
    me_dp, me_mp = lax.axis_index("dp"), lax.axis_index("mp")
    parity = lax.rem(me_mp, 2)
    size = shard.shape[0]
    enter(n_dp, n_mp, me_dp, me_mp, exchange)
    partial = ins[0]
    total = scatter_sum(
        partial, landed, rs_send, rs_recv, me_mp, n_mp, flipped if kind == "embed" else same
    )
    if kind == "embed":
        values = total
    elif kind in ("mid", "to_cols"):
        values = own_rows(ins[1], me_mp, size) + total
    elif kind == "to_rows":
        values = norm_back(
            own_rows(ins[1], me_mp, size), total / math.sqrt(shard.shape[1]), ins[2][...].astype(FL)
        )
    else:
        values = own_rows(ins[3], me_mp, size) + norm_back(
            own_rows(ins[1], me_mp, size), total, ins[2][...].astype(FL)
        )
    if exchange:
        wide, outgo, income, a2a_send, a2a_recv = scratch[6:]
        shift_in = 1 - parity if kind == "embed" else 0
        shift_out = 1 - parity if kind == "d_embed" else 0
        values = swap_tokens(
            values, wide, outgo, income, a2a_send, a2a_recv, me_dp, n_dp, shift_out, shift_in
        )
        if kind == "embed":
            first = lax.broadcasted_iota(jnp.int32, values.shape, 0) + parity == 0
            values = jnp.where(first, ins[1][...].astype(FL), values)
        if kind == "d_embed":
            keep = jnp.where((me_dp == n_dp - 1) & (parity == 0), 0.0, 1.0)
            values = values * keep
    shard[...] = values.astype(BF)
    slot = flipped(me_mp) if kind == "d_embed" else me_mp
    gather_slots(shard, full, ag_send, ag_recv, me_mp, n_mp, slot)


IDS = {"embed": 1, "mid": 2, "to_cols": 3, "to_rows": 4, "d_mid": 5, "d_embed": 6, "totals": 7}


def step(kind, n_dp, n_mp, *args):
    tokens, width = args[0].shape
    size = tokens // n_mp
    dma = pltpu.SemaphoreType.DMA
    scratch = [
        pltpu.VMEM((n_mp, size, width), BF),
        pltpu.VMEM((size, width), BF),
        dma((n_mp,)),
        dma((n_mp,)),
        dma((n_mp,)),
        dma((n_mp,)),
    ]
    if kind in ("embed", "to_cols", "to_rows", "d_embed"):
        parts = width // LANES
        scratch += [
            pltpu.VMEM((size * parts, LANES), FL),
            pltpu.VMEM((size, parts, LANES), BF),
            pltpu.VMEM((size, parts, LANES), BF),
            dma((n_dp,)),
            dma((n_dp,)),
        ]
    vmem = pl.BlockSpec(memory_space=pltpu.VMEM)
    return pl.pallas_call(
        functools.partial(step_kernel, kind, n_dp, n_mp),
        out_shape=jax.ShapeDtypeStruct((tokens, width), BF),
        in_specs=[vmem] * len(args),
        out_specs=vmem,
        scratch_shapes=scratch,
        compiler_params=pltpu.CompilerParams(collective_id=IDS[kind], has_side_effects=True),
        name="step_" + kind,
    )(*args)


def totals_kernel(n_mp, mine, out, landed, send, recv):
    me = lax.axis_index("mp")
    enter(1, n_mp, 0, me, False)
    copies = []
    for off in range(1, n_mp):
        copy = pltpu.make_async_remote_copy(
            src_ref=mine,
            dst_ref=landed.at[off],
            send_sem=send.at[off],
            recv_sem=recv.at[off],
            device_id={"mp": lax.rem(me + off, n_mp)},
            device_id_type=MESH,
        )
        copy.start()
        copies.append(copy)
    total = mine[...]
    for off, copy in enumerate(copies, 1):
        copy.wait()
        total = total + landed[off]
    out[...] = total


def totals(values, n_mp):
    vmem = pl.BlockSpec(memory_space=pltpu.VMEM)
    dma = pltpu.SemaphoreType.DMA
    return pl.pallas_call(
        functools.partial(totals_kernel, n_mp),
        out_shape=jax.ShapeDtypeStruct(values.shape, FL),
        in_specs=[vmem],
        out_specs=vmem,
        scratch_shapes=[pltpu.VMEM((n_mp, *values.shape), FL), dma((n_mp,)), dma((n_mp,))],
        compiler_params=pltpu.CompilerParams(collective_id=IDS["totals"], has_side_effects=True),
        name="step_totals",
    )(values)


def normalize(values, gain):
    floats = values.astype(FL)
    return (floats / rms_of(floats) * gain.astype(FL)).astype(BF)


def dot(spec, a, b):
    return jnp.einsum(spec, a, b, preferred_element_type=FL)


def local(
    token_ids,
    fanout,
    table_of_column,
    embed_table,
    start_vector,
    gain_attn,
    gain_mlp,
    gain_final,
    w_qkv,
    w_out,
    w_gate,
    w_up,
    w_down,
):
    me_mp = lax.axis_index("mp")
    n_mp = lax.axis_size("mp")
    n_dp = lax.axis_size("dp")
    own_cols, vocab_part, width = embed_table.shape
    row_count = token_ids.shape[0]
    rows = row_count // n_dp
    tokens = row_count * own_cols
    col_count = own_cols * n_dp
    head_cols = w_qkv.shape[2]
    heads = head_cols // HS

    def row(vector):
        return vector.reshape(1, width)

    ids = token_ids.reshape(n_dp, rows, own_cols).transpose(1, 2, 0)
    local_ids = ids - me_mp * vocab_part
    hit = local_ids[..., None] == jnp.arange(vocab_part, dtype=jnp.int32)
    onehot = hit.astype(BF)
    picked = dot("rpkv,pvd->rpkd", onehot, embed_table).astype(BF).reshape(tokens, width)
    resid_in = step("embed", n_dp, n_mp, picked, row(start_vector))

    norm_attn = normalize(resid_in, gain_attn)
    qkv = dot("nd,dtx->ntx", norm_attn, w_qkv).astype(BF)
    split = qkv.reshape(rows, col_count, 3, heads, HS)
    queries, key_rows, value_rows = split[:, :, 0], split[:, :, 1], split[:, :, 2]
    score_raw = dot("rqhe,rkhe->rhqk", queries, key_rows) / math.sqrt(HS)
    score = ATTN_CAP * jnp.tanh(score_raw / ATTN_CAP)
    place = jnp.arange(col_count, dtype=jnp.int32)
    col_index = own_cols * (place % n_dp) + place // n_dp
    causal = col_index[:, None] >= col_index[None, :]
    exp_score = jnp.where(causal, jnp.exp(score), 0.0)
    attn_prob = exp_score / jnp.sum(exp_score, axis=-1, keepdims=True)
    prob_b = attn_prob.astype(BF)
    attn_out = dot("rhqk,rkhe->rqhe", prob_b, value_rows).astype(BF).reshape(tokens, head_cols)
    mixed = dot("nj,dj->nd", attn_out, w_out).astype(BF)
    resid_mid = step("mid", n_dp, n_mp, mixed, resid_in)

    norm_mlp = normalize(resid_mid, gain_mlp)
    gate_pre = dot("nd,df->nf", norm_mlp, w_gate)
    up_proj = dot("nd,df->nf", norm_mlp, w_up)
    hidden = (jax.nn.silu(gate_pre) * up_proj).astype(BF)
    down = dot("nf,df->nd", hidden, w_down).astype(BF)
    out_cols = step("to_cols", n_dp, n_mp, down, resid_mid)

    norm_final = normalize(out_cols, gain_final).reshape(rows, own_cols, n_dp, width)
    width_root = math.sqrt(width)
    logit_raw = dot("rpkd,pvd->rpkv", norm_final, embed_table) / width_root
    capped = LOGIT_CAP * jnp.tanh(logit_raw / LOGIT_CAP)
    exp_logit = jnp.exp(capped)
    sums = jnp.stack(
        [
            jnp.sum(exp_logit, axis=-1).reshape(tokens),
            jnp.sum(jnp.where(hit, capped, 0.0), axis=-1).reshape(tokens),
        ]
    ).reshape(2 * tokens // LANES, LANES)
    exp_total, target_logit = totals(sums, n_mp).reshape(2, rows, own_cols, n_dp)
    nll = jnp.log(exp_total) - target_logit
    select = table_of_column[None, :, None] == jnp.arange(TABLES, dtype=jnp.int32)[None, None, :]
    counts = jnp.sum(jnp.where(select, fanout[:, None, :], 0), axis=-1).astype(FL)
    row_scale = (1.0 / (counts * row_count)).reshape(n_dp, rows, own_cols).transpose(1, 2, 0)
    ratio = capped / LOGIT_CAP
    d_logit = (
        (exp_logit / exp_total[..., None] - hit.astype(FL))
        * row_scale[..., None]
        * (1.0 - ratio * ratio)
    ).astype(BF)
    d_final = dot("rpkv,pvd->rpkd", d_logit, embed_table).astype(BF).reshape(tokens, width)
    table_grad = dot("rpkv,rpkd->pvd", d_logit, norm_final) / width_root
    d_out = step("to_rows", n_dp, n_mp, d_final, out_cols, row(gain_final))

    d_hidden = dot("nd,df->nf", d_out, w_down)
    sigmoid_gate = jax.nn.sigmoid(gate_pre)
    d_gate = (d_hidden * up_proj * sigmoid_gate * (1.0 + gate_pre * (1.0 - sigmoid_gate))).astype(BF)
    d_up = (d_hidden * gate_pre * sigmoid_gate).astype(BF)
    d_norm_mlp = (dot("nf,df->nd", d_gate, w_gate) + dot("nf,df->nd", d_up, w_up)).astype(BF)
    mlp_terms = jnp.concatenate(
        [
            dot("nd,nf->df", norm_mlp, d_gate),
            dot("nd,nf->df", norm_mlp, d_up),
            dot("nd,nf->df", d_out, hidden),
        ],
        axis=1,
    )
    mlp_sum = lax.psum_scatter(mlp_terms, "dp", scatter_dimension=0, tiled=True)
    d_mid = step("d_mid", n_dp, n_mp, d_norm_mlp, resid_mid, row(gain_mlp), d_out)

    d_attn = dot("nd,dj->nj", d_mid, w_out).astype(BF).reshape(rows, col_count, heads, HS)
    d_prob = dot("rqhe,rkhe->rhqk", d_attn, value_rows)
    ratio_s = score / ATTN_CAP
    d_score = attn_prob * (d_prob - jnp.sum(attn_prob * d_prob, axis=-1, keepdims=True))
    d_scaled = (d_score * (1.0 - ratio_s * ratio_s) / math.sqrt(HS)).astype(BF)
    d_query = dot("rhqk,rkhe->rqhe", d_scaled, key_rows)
    d_key = dot("rhqk,rqhe->rkhe", d_scaled, queries)
    d_value = dot("rhqk,rqhe->rkhe", prob_b, d_attn)
    d_qkv = (
        jnp.stack([d_query, d_key, d_value], axis=2).reshape(tokens, 3, head_cols).astype(BF)
    )
    d_norm_attn = dot("ntx,dtx->nd", d_qkv, w_qkv).astype(BF)
    attn_terms = jnp.concatenate(
        [
            dot("nd,ntx->dtx", norm_attn, d_qkv).reshape(width, 3 * head_cols),
            dot("nd,nj->dj", d_mid, attn_out),
        ],
        axis=1,
    )
    attn_sum = lax.psum_scatter(attn_terms, "dp", scatter_dimension=0, tiled=True)
    d_embed = step("d_embed", n_dp, n_mp, d_norm_attn, resid_in, row(gain_attn), d_mid)
    table_grad = table_grad + dot(
        "rpkv,rpkd->pvd", onehot, d_embed.reshape(rows, own_cols, n_dp, width)
    )

    ff = w_gate.shape[1]
    qkv_width = 3 * head_cols
    return (
        nll.transpose(2, 0, 1).reshape(row_count, own_cols),
        table_grad,
        attn_sum[:, :qkv_width].reshape(attn_sum.shape[0], 3, head_cols),
        attn_sum[:, qkv_width:],
        mlp_sum[:, :ff],
        mlp_sum[:, ff : 2 * ff],
        mlp_sum[:, 2 * ff :],
    )


def solution(mesh):
    return jax.shard_map(
        local,
        mesh=mesh,
        in_specs=(
            P(None, "dp"),
            P(),
            P("dp"),
            P("dp", "mp", None),
            P(),
            P(),
            P(),
            P(),
            P(None, None, "mp"),
            P(None, "mp"),
            P(None, "mp"),
            P(None, "mp"),
            P(None, "mp"),
        ),
        out_specs=(
            P(None, "dp"),
            P("dp", "mp", None),
            P("dp", None, "mp"),
            P("dp", "mp"),
            P("dp", "mp"),
            P("dp", "mp"),
            P("dp", "mp"),
        ),
        check_vma=False,
    )
```

time: 728 us -> 464 us (0.64)
  blocking collectives: 230 us -> 0 us
  Pallas kernels: 0 us -> 176 us
  waiting for transfers between devices: 364 us -> 207 us
  starting transfers between devices: 30.4 us -> 0.26 us
  matrix products: 46 us -> 22.6 us
    pallas_call x0 -> x7, Pallas kernels: none -> 176 us  [the longest x6 167 us: step(): pl.pallas_call(functools.partial(step_kernel, kind, n_dp, n_mp), out_shap...]
    reduce_scatter x5 -> x0, waiting for transfers between devices: 170 us -> none  [feature_sum(): return lax.psum_scatter(term, 'mp', scatter_dimension=2, tiled=True)]
    all_gather x6 -> x0, blocking collectives: 161 us -> none  [gather_features(): return lax.all_gather(values, 'mp', axis=2, tiled=True)]
    unnamed x8 -> x4, waiting for transfers between devices: 90.5 us -> 207 us
    psum x1 -> x0, waiting for transfers between devices: 76.1 us -> none  [local(): d_final = lax.psum(d_final_part, 'mp')]
    psum x3 -> x0, blocking collectives: 49.6 us -> none  [the longest x2 31.7 us: local(): lax.psum((jnp.sum(exp_logit, axis=-1), jnp.sum(capped * onehot_f, axis=-1...]
    all_to_all x3 -> x0, starting transfers between devices: 30 us -> none  [the longest x2 20 us: rows_to_cols(): return lax.all_to_all(values, 'dp', split_axis=1, concat_axis=0, tiled=True)]
    all_to_all x3 -> x0, waiting for transfers between devices: 27.1 us -> none  [the longest x2 18.7 us: rows_to_cols(): return lax.all_to_all(values, 'dp', split_axis=1, concat_axis=0, tiled=True)]
  transfers between devices with their start and end apart: 10 -> 2, of which waited for: 10 -> 2; matrix products, arithmetic and copies ran while one was open for 5% -> 4% of each run, Pallas kernels for 0% -> 7%
where the time goes in v1:
time: 464 us; the launch traced here: 463 us
  waiting for transfers between devices  207 us (45%)
  Pallas kernels  176 us (38%)
  local copies, waits for them, and re-layouts  29.6 us (6%)
  matrix products  22.6 us (5%)
  between operations  14.7 us (3%)
  other arithmetic  12.8 us (3%)
    unnamed x4, waiting for transfers between devices  207 us
    pallas_call x6, Pallas kernels, step(): pl.pallas_call(functools.partial(step_kernel, kind, n_dp, n_mp), out_shap...  167 us
    dot_general x26, matrix products, dot(): return jnp.einsum(spec, a, b, preferred_element_type=FL)  22.6 us
    unnamed x69, local copies, waits for them, and re-layouts  15.1 us
  transfers between devices with their start and end apart: 2, of which 2 were waited for; matrix products, arithmetic and copies ran while one was open for 4% of the time, Pallas kernels for 7%

profile of v1, /device:TPU:2, one launch (start us, length us, event | category | flops | bytes accessed | tf_op | source)
XLA Modules:
  0.0 463.0 jit_solution(17922455756537816602)
XLA Ops:
  8.1 1.3 reshape.192.refs_2_
  15.9 1.4 fusion.5
  18.2 32.8 %step_embed.1.refs_1_ = bf16[256,1024]{1,0:T(8,128)(2,1)} custom-call(bf16[256,1024]{1,0:T(8,128)(2,1)} %bitcast.125, bf16[1,1024]{1,0:T(2,128)(2,1)} %reshape.184.refs_1_), custom_call_target="tpu_custom_call" | custom-call | tf_op jit(solution)/shard_map/step_embed/pallas_call | solution.py:210
  52.2 1.5 convolution_convert_fusion.4
  56.6 20.4 %step_mid.1.refs_1_ = bf16[256,1024]{1,0:T(8,128)(2,1)} custom-call(bf16[256,1024]{1,0:T(8,128)(2,1)} %convolution_convert_fusion.3.refs_0_, bf16[256,1024]{1,0:T(8,128)(2,1)} %step_embed.1.refs_1_), custom_call_target="tpu_custom_call" | custom-call | tf_op jit(solution)/shard_map/step_mid/pallas_call | solution.py:210
  78.2 1.6 fusion.80
  79.9 1.3 multiply_convert_fusion.2
  81.9 1.3 convolution_convert_fusion.refs_0_
  83.2 30.7 %step_to_cols.1.refs_1_ = bf16[256,1024]{1,0:T(8,128)(2,1)} custom-call(bf16[256,1024]{1,0:T(8,128)(2,1)} %convolution_convert_fusion.refs_0_, bf16[256,1024]{1,0:T(8,128)(2,1)} %step_mid.1.refs_1_), custom_call_target="tpu_custom_call" | custom-call | tf_op jit(solution)/shard_map/step_to_cols/pallas_call | solution.py:210
  118.5 8.9 %step_totals.1 = f32[4,128]{1,0:T(4,128)} custom-call(f32[4,128]{1,0:T(4,128)} %reshape.188.mine), custom_call_target="tpu_custom_call" | custom-call | tf_op jit(solution)/shard_map/step_totals/pallas_call | solution.py:246
  129.5 30.2 %step_to_rows.1.refs_3_ = bf16[256,1024]{1,0:T(8,128)(2,1)} custom-call(bf16[256,1024]{1,0:T(8,128)(2,1)} %bitcast.121, bf16[256,1024]{1,0:T(8,128)(2,1)} %step_to_cols.1.refs_1_, bf16[1,1024]{1,0:T(2,128)(2,1)} %reshape.191.refs_2_), custom_call_target="tpu_custom_call" | custom-call | tf_op jit(solution)/shard_map/step_to_rows/pallas_call | solution.py:210
  159.7 1.8 multiply_convert_fusion
  164.2 21.2 %step_d_mid.1.refs_3_ = bf16[256,1024]{1,0:T(8,128)(2,1)} custom-call(bf16[256,1024]{1,0:T(8,128)(2,1)} %fusion.3.refs_0_, bf16[256,1024]{1,0:T(8,128)(2,1)} %step_mid.1.refs_1_, bf16[1,1024]{1,0:T(2,128)(2,1)} %reshape.192.refs_2_, bf16[256,1024]{1,0:T(8,128)(2,1)} %step_to_rows.1.refs_3_), custom_call_target="tpu_custom_call" | custom-call | tf_op jit(solution)/shard_map/step_d_mid/pallas_call | solution.py:210
  185.5 1.3 convolution_convert_fusion.9
  191.8 1.8 copy.226
  196.7 3.2 pad_maximum_fusion
  200.0 6.6 %copy.228 = f32[1024,1536]{1,0:T(8,128)} copy(f32[1024,1536]{0,1:T(8,128)} %pad_maximum_fusion) | data formatting | bytes 12582912
  209.8 31.6 %step_d_embed.1 = bf16[256,1024]{1,0:T(8,128)(2,1)} custom-call(bf16[256,1024]{1,0:T(8,128)(2,1)} %fusion.4.refs_0_, bf16[256,1024]{1,0:T(8,128)(2,1)} %step_embed.1.refs_1_, bf16[1,1024]{1,0:T(2,128)(2,1)} %reshape.194.refs_2_, bf16[256,1024]{1,0:T(8,128)(2,1)} %step_d_mid.1.refs_3_), custom_call_target="tpu_custom_call" | custom-call | tf_op jit(solution)/shard_map/step_d_embed/pallas_call | solution.py:210
  241.4 1.5 convolution_bitcast_fusion
  242.9 1.5 fusion.2
  244.4 70.6 %reduce-scatter.7.cloned.1.call-done = f32[32,512]{1,0:T(8,128)} async-done(((f32[1024,512]{1,0:T(8,128)}), f32[32,512]{1,0:T(8,128)}) %reduce-scatter.7.cloned.1.call-update) | async-done | bytes 65552
  316.6 1.3 slice.38
  318.0 136.6 %reduce-scatter.9.cloned.1.call-done = f32[32,1536]{1,0:T(8,128)} async-done(((f32[1024,1536]{1,0:T(8,128)}), f32[32,1536]{1,0:T(8,128)}) %reduce-scatter.9.cloned.1.call-update) | async-done | bytes 196624
  454.6 1.6 fusion.83
  (141 shorter events, 36.4 us)
Async XLA Ops:
  7.2 74.7 %copy-start = (bf16[1024,512]{1,0:T(8,128)(2,1)S(1)}, bf16[1024,512]{1,0:T(8,128)(2,1)}, u32[]{:S(2)}) copy-start(bf16[1024,512]{1,0:T(8,128)(2,1)} %param.25) | copy-start | bytes 3145732
  7.2 45.0 %copy-start.16 = (bf16[1024,3,128]{2,0,1:T(8,128)(2,1)S(1)}, bf16[1024,3,128]{2,0,1:T(8,128)(2,1)}, u32[]{:S(2)}) copy-start(bf16[1024,3,128]{2,0,1:T(8,128)(2,1)} %param.21) | copy-start | bytes 2359300
  7.2 307.8 %reduce-scatter.7.cloned.1.call-start = ((), (), s32[]{:S(2)}) async-start(), calls=%async_computation.2 | async-start | bytes 2162688
  53.8 1.7 copy-start.11
  54.7 22.2 %copy-start.27 = (f32[4,2,64,64]{2,3,1,0:T(8,128)}, f32[4,2,64,64]{2,3,1,0:T(8,128)S(1)}, u32[]{:S(2)}) copy-start(f32[4,2,64,64]{2,3,1,0:T(8,128)S(1)} %get-tuple-element.64) | copy-start | bytes 393220
  55.0 23.2 %copy-start.10 = (bf16[1024,512]{1,0:T(8,128)(2,1)S(1)}, bf16[1024,512]{1,0:T(8,128)(2,1)}, u32[]{:S(2)}) copy-start(bf16[1024,512]{1,0:T(8,128)(2,1)} %param.23) | copy-start | bytes 3145732
  78.2 1.7 copy-start.1
  78.2 1.7 copy-start.12
  79.9 1.3 copy-start.29
  81.9 35.4 %copy-start.6 = (bf16[2,128,1024]{2,1,0:T(8,128)(2,1)S(1)}, bf16[2,128,1024]{2,1,0:T(8,128)(2,1)}, u32[]{:S(2)}) copy-start(bf16[2,128,1024]{2,1,0:T(8,128)(2,1)} %param.16) | copy-start | bytes 1572868
  128.7 31.1 %copy-start.30 = (f32[256,512]{1,0:T(8,128)S(1)}, f32[256,512]{1,0:T(8,128)}, u32[]{:S(2)}) copy-start(f32[256,512]{1,0:T(8,128)} %copy-done.29) | copy-start | bytes 1572868
  161.5 2.7 copy-start.18
  161.5 1.4 copy-start.13
  164.2 23.1 %copy-start.28 = (f32[4,2,64,64]{2,3,1,0:T(8,128)S(1)}, f32[4,2,64,64]{2,3,1,0:T(8,128)}, u32[]{:S(2)}) copy-start(f32[4,2,64,64]{2,3,1,0:T(8,128)} %copy-done.27) | copy-start | bytes 393220
  164.2 23.3 %copy-start.25 = (bf16[4,64,1,2,64]{4,3,1,0,2:T(2,128)(2,1)S(1)}, bf16[4,64,1,2,64]{4,3,1,0,2:T(2,128)(2,1)}, u32[]{:S(2)}) copy-start(bf16[4,64,1,2,64]{4,3,1,0,2:T(2,128)(2,1)} %copy-done.24) | copy-start | bytes 196612
  187.5 1.1 copy-start.4
  188.6 2.0 copy-start.3
  190.6 1.0 copy-start.9
  193.6 1.1 copy-start.15
  193.6 1.6 copy-start.2
  193.6 1.6 copy-start.21
  193.6 260.9 %reduce-scatter.9.cloned.1.call-start = ((), (), s32[]{:S(2)}) async-start(), calls=%async_computation.3 | async-start | bytes 6488064
  206.5 2.0 copy-start.17
  209.8 33.0 %copy-start.8 = (bf16[256,1024]{1,0:T(8,128)(2,1)S(1)}, bf16[256,1024]{1,0:T(8,128)(2,1)}, u32[]{:S(2)}) copy-start(bf16[256,1024]{1,0:T(8,128)(2,1)} %copy-done.7) | copy-start | bytes 1572868
  (9 other events, 7.3 us)
Sparse Core Ops, SparseCore 0:
  193.8 121.1 reduce-scatter.6
  319.3 135.2 reduce-scatter.8

commit v2 on v0

v2 whole, which is shorter than its diff:
```python
import functools
import math
import types

import jax
import jax.numpy as jnp
from jax import lax
from jax.experimental import pallas as pl
from jax.experimental.pallas import tpu as pltpu
from jax.sharding import PartitionSpec as P

HS = 64
TABLES = 16
EPS = 1e-05
ATTN_CAP = 50.0
LOGIT_CAP = 30.0
MESH = pl.DeviceIdType.MESH
FL = jnp.float32
BF = jnp.bfloat16
LANES = 128
HBM = "_hbm"
MLP = "mlp_ring_"
ATTN = "attn_ring_"

EMBED, MID, COLS, ROWS, D_MID, D_EMBED = range(6)


def nn(a, b):
    return lax.dot_general(a, b, (((1,), (0,)), ((), ())), preferred_element_type=FL)


def nt(a, b):
    return lax.dot_general(a, b, (((1,), (1,)), ((), ())), preferred_element_type=FL)


def tn(a, b):
    return lax.dot_general(a, b, (((0,), (0,)), ((), ())), preferred_element_type=FL)


def rms_of(floats):
    return jnp.sqrt(jnp.mean(floats * floats, axis=-1, keepdims=True) + EPS)


def norm_back(floats, d_norm, gains):
    rms = rms_of(floats)
    total = jnp.sum(gains * d_norm * floats, axis=-1, keepdims=True)
    return gains * d_norm / rms - floats * total / (floats.shape[-1] * rms * rms * rms)


def block(index, size):
    return pl.ds(pl.multiple_of(index * size, size), size)


class Ring:
    def __init__(self, me, ref, prefix):
        for name, value in vars(ref).items():
            if name.startswith(prefix):
                setattr(self, name.removeprefix(prefix), value)
        self.me = me
        self.z, self.y, self.core = me // 4, lax.rem(me // 2, 2), lax.rem(me, 2)
        self.length = self.pair_out.shape[0]
        self.half = self.terms.shape[2] // 2
        self.seen = set()

    def chunk(self, off):
        return lax.rem(self.z + off, self.length)

    def copy(self, src, dst, send, recv, peer):
        return pltpu.make_async_remote_copy(
            src_ref=src,
            dst_ref=dst,
            send_sem=send,
            recv_sem=recv,
            device_id={"dp": peer},
            device_id_type=MESH,
        )

    def pair_copy(self, off):
        peer = self.me + 1 - 2 * self.core
        sems = self.pair_sems
        return self.copy(
            self.pair_out.at[off], self.pair_in.at[off], sems.at[0, off], sems.at[1, off], peer
        )

    def pair(self):
        n = self.length
        order = [off for near in range(1, n // 2) for off in (n - near, near)] + [n // 2, 0]
        for off in order:
            base = self.chunk(off) * 4
            for y in range(2):
                self.pair_out[off, y] = self.terms[base + 2 * y + 1 - self.core].astype(BF)
            self.pair_copy(off).start()

    def mine(self, off, y, side):
        if off not in self.seen:
            self.seen.add(off)
            self.pair_copy(off).wait_recv()
        cols = slice(side * self.half, (side + 1) * self.half)
        own = self.terms[self.chunk(off) * 4 + 2 * y + self.core, :, cols]
        return own + self.pair_in[off, y, :, cols].astype(FL)

    def hop(self, side, t):
        near = lax.rem(self.z + (1 if side == 0 else self.length - 1), self.length)
        return self.copy(
            self.hop_out.at[side, t],
            self.hop_in.at[side, t],
            self.hop_send.at[side, t],
            self.hop_recv.at[side, t],
            near * 4 + lax.rem(self.me, 4),
        )

    def step(self, t):
        for side in range(2):
            off = self.length - 1 - t if side == 0 else 1 + t
            if t > 0:
                self.hop(side, t - 1).wait_recv()
            for y in range(2):
                value = self.mine(off, y, side)
                if t > 0:
                    value = value + self.hop_in[side, t - 1, y].astype(FL)
                self.hop_out[side, t, y] = value.astype(BF)
            self.hop(side, t).start()

    def y_copy(self):
        peer = self.me + 2 - 4 * self.y
        return self.copy(self.y_out, self.y_in, self.y_sems.at[0], self.y_sems.at[1], peer)

    def cross(self):
        t = self.length - 2
        for side in range(2):
            self.hop(side, t).wait_recv()
            cols = slice(side * self.half, (side + 1) * self.half)
            for y in range(2):
                self.last[y, :, cols] = self.mine(0, y, side) + self.hop_in[side, t, y].astype(FL)
        self.y_out[...] = self.last[1 - self.y].astype(BF)
        self.y_copy().start()

    def result(self):
        self.y_copy().wait_recv()
        return self.last[self.y] + self.y_in[...].astype(FL)

    def drain(self):
        for off in range(self.length):
            self.pair_copy(off).wait_send()
        for side in range(2):
            for t in range(self.length - 1):
                self.hop(side, t).wait_send()
        self.y_copy().wait_send()


def window_kernel(n_dp, n_mp, names, *refs):
    ref = types.SimpleNamespace(**dict(zip(names, refs)))
    me_dp, me_mp = lax.axis_index("dp"), lax.axis_index("mp")
    parity, row = lax.rem(me_mp, 2), me_mp // 2
    part, land, full = ref.part, ref.land, ref.full
    tokens, width = part.shape[1:]
    size = tokens // n_mp
    half = tokens // 2
    parts = width // LANES
    root = math.sqrt(width)
    group_rows = n_mp // 2

    loads = types.SimpleNamespace()
    for slot, name in enumerate(name for name in names if name.endswith(HBM)):
        here = name.removesuffix(HBM)
        copy = pltpu.make_async_copy(getattr(ref, name), getattr(ref, here), ref.load_sem.at[slot])
        copy.start()
        setattr(loads, here, copy)

    barrier = pltpu.get_barrier_semaphore()
    for axis, me, count in (("mp", me_mp, n_mp), ("dp", me_dp, n_dp)):

        def greet(off, carry, axis=axis, me=me, count=count):
            pl.semaphore_signal(
                barrier, inc=1, device_id={axis: lax.rem(me + off, count)}, device_id_type=MESH
            )
            return carry

        lax.fori_loop(1, count, greet, 0)

    def row_slot(mp):
        return mp

    def col_slot(mp):
        return lax.rem(mp, 2) * group_rows + mp // 2

    def other_col_slot(mp):
        return (1 - lax.rem(mp, 2)) * group_rows + mp // 2

    offsets = [off for _, off in sorted((-min(off, n_mp - off), off) for off in range(1, n_mp))]

    def rs_copy(stage, off, slot_of):
        peer = lax.rem(me_mp + off, n_mp)
        return pltpu.make_async_remote_copy(
            src_ref=part.at[stage, block(slot_of(peer), size)],
            dst_ref=land.at[stage, off],
            send_sem=ref.rs_send.at[stage],
            recv_sem=ref.rs_recv.at[stage, off],
            device_id={"mp": peer},
            device_id_type=MESH,
        )

    def rs_start(stage, slot_of):
        for off in offsets:
            rs_copy(stage, off, slot_of).start()

    def rs_finish(stage, slot_of):
        total = part[stage, block(slot_of(me_mp), size), :].astype(FL)
        for off in reversed(offsets):
            rs_copy(stage, off, slot_of).wait_recv()
            total = total + land[stage, off].astype(FL)
        return total

    def ag_copy(stage, off, slot):
        where = full.at[stage, block(slot, size)]
        return pltpu.make_async_remote_copy(
            src_ref=where,
            dst_ref=where,
            send_sem=ref.ag_send.at[stage],
            recv_sem=ref.ag_recv.at[stage, off],
            device_id={"mp": lax.rem(me_mp + off, n_mp)},
            device_id_type=MESH,
        )

    def ag_start(stage, slot, values):
        full[stage, block(slot, size), :] = values.astype(BF)
        for off in offsets:
            ag_copy(stage, off, slot).start()

    def ag_finish(stage, slot):
        for off in offsets:
            ag_copy(stage, off, slot).wait_recv()

    wide, outgo, income = ref.wide, ref.outgo, ref.income

    def a2a_copy(which, off, shift_out, shift_in):
        peer = lax.rem(me_dp + off, n_dp)
        return pltpu.make_async_remote_copy(
            src_ref=outgo.at[which, lax.rem(peer + shift_out, n_dp)],
            dst_ref=income.at[which, lax.rem(me_dp + shift_in, n_dp)],
            send_sem=ref.a2a_send.at[which],
            recv_sem=ref.a2a_recv.at[which],
            device_id={"dp": peer},
            device_id_type=MESH,
        )

    def a2a_all(which):
        return pltpu.make_async_remote_copy(
            src_ref=outgo.at[which, pl.ds(0, n_dp - 1)],
            dst_ref=income.at[which, pl.ds(0, n_dp - 1)],
            send_sem=ref.a2a_send.at[which],
            recv_sem=ref.a2a_recv.at[which],
            device_id={"dp": lax.rem(me_dp + 1, n_dp)},
            device_id_type=MESH,
        )

    def a2a_start(which, values, shift_out, shift_in):
        for i in range(parts):
            wide[pl.ds(i, size, stride=parts), :] = values[:, i * LANES : (i + 1) * LANES]
        outgo[which] = wide[...].reshape(size, parts, LANES).astype(BF)

        def start(off, carry):
            a2a_copy(which, off, shift_out, shift_in).start()
            return carry

        lax.fori_loop(1, n_dp, start, 0)

    def a2a_finish(which, shift_out, shift_in):
        a2a_all(which).wait_recv()
        income[which, lax.rem(me_dp + shift_in, n_dp)] = outgo[
            which, lax.rem(me_dp + shift_out, n_dp)
        ]
        wide[...] = income[which].astype(FL).reshape(size * parts, LANES)
        return jnp.concatenate(
            [wide[pl.ds(i, size, stride=parts), :] for i in range(parts)], axis=1
        )

    def own(stage, slot):
        return full[stage, block(slot, size), :].astype(FL)

    def normalize(stage, gain, out):
        @pl.loop(0, n_mp)
        def _(i):
            floats = full[stage, block(i, size), :].astype(FL)
            out[block(i, size), :] = (floats / rms_of(floats) * gain[...].astype(FL)).astype(BF)

    def weight_terms(left, right, out, cols):
        @pl.loop(0, width // LANES)
        def _(i):
            value = tn(left[:, block(i, LANES)], right[...])
            out[pl.ds(i * 4, 4), :, cols] = value.reshape(4, LANES // 4, value.shape[1])

    vocab = lax.broadcasted_iota(jnp.int32, (LANES, half), 0)
    loads.table_in.wait()
    table_in = ref.table_in

    def hits(p):
        return vocab == ref.ids[p : p + 1, :]

    for p in range(2):
        picked = tn(hits(p).astype(FL).astype(BF), table_in[p])
        part[EMBED, p * half : (p + 1) * half, :] = picked.astype(BF)
    pl.semaphore_wait(barrier, n_mp - 1 + n_dp - 1)
    rs_start(EMBED, other_col_slot)
    a2a_start(0, rs_finish(EMBED, other_col_slot), 0, 1 - parity)
    values = a2a_finish(0, 0, 1 - parity)
    first = lax.broadcasted_iota(jnp.int32, values.shape, 0) + parity == 0
    values = jnp.where(first, ref.start[...].astype(FL), values)
    ag_start(EMBED, me_mp, values)
    ag_finish(EMBED, me_mp)

    norm_attn, qkv, attn_out = ref.norm_attn, ref.qkv, ref.attn_out
    score, prob = ref.score, ref.prob
    normalize(EMBED, ref.gain_attn, norm_attn)
    loads.w_qkv.wait()
    qkv[...] = nn(norm_attn[...], ref.w_qkv[...]).astype(BF)
    head_cols = attn_out.shape[1]
    lane = lax.broadcasted_iota(jnp.int32, (1, head_cols), 1)
    head_masks = [
        ((lane >= h * HS) & (lane < (h + 1) * HS)).astype(FL).astype(BF)
        for h in range(head_cols // HS)
    ]
    queries = qkv[:, :head_cols]
    key_rows = qkv[:, head_cols : 2 * head_cols]
    value_rows = qkv[:, 2 * head_cols :]
    cols_in_row = tokens // group_rows
    at = lax.broadcasted_iota(jnp.int32, (tokens, tokens), 0)
    to = lax.broadcasted_iota(jnp.int32, (tokens, tokens), 1)

    def column(token):
        inside = lax.rem(token, cols_in_row)
        return 2 * lax.rem(inside, n_dp) + inside // n_dp

    seen = (at // cols_in_row == to // cols_in_row) & (column(at) >= column(to))
    mixed = jnp.zeros((tokens, head_cols), FL)
    for h, mask in enumerate(head_masks):
        raw = nt(queries * mask, key_rows) / math.sqrt(HS)
        capped = ATTN_CAP * jnp.tanh(raw / ATTN_CAP)
        weights = jnp.where(seen, jnp.exp(capped), 0.0)
        weights = weights / jnp.sum(weights, axis=-1, keepdims=True)
        score[h] = capped
        prob[h] = weights
        mixed = mixed + nn(weights.astype(BF), value_rows * mask)
    attn_out[...] = mixed.astype(BF)
    loads.w_out.wait()
    part[MID] = nt(attn_out[...], ref.w_out[...]).astype(BF)
    rs_start(MID, row_slot)
    ag_start(MID, me_mp, own(EMBED, me_mp) + rs_finish(MID, row_slot))
    ag_finish(MID, me_mp)

    norm_mlp, gate_pre, up_proj, hidden = (
        ref.norm_mlp,
        ref.gate_pre,
        ref.up_proj,
        ref.hidden,
    )
    normalize(MID, ref.gain_mlp, norm_mlp)
    loads.w_gate.wait()
    gate_pre[...] = nn(norm_mlp[...], ref.w_gate[...])
    loads.w_up.wait()
    up_proj[...] = nn(norm_mlp[...], ref.w_up[...])

    @pl.loop(0, n_mp)
    def _(i):
        where = block(i, size)
        gate = gate_pre[where, :]
        hidden[where, :] = (gate * jax.nn.sigmoid(gate) * up_proj[where, :]).astype(BF)

    loads.w_down.wait()
    part[COLS] = nt(hidden[...], ref.w_down[...]).astype(BF)
    rs_start(COLS, row_slot)
    a2a_start(1, own(MID, me_mp) + rs_finish(COLS, row_slot), 0, 0)
    ag_start(COLS, col_slot(me_mp), a2a_finish(1, 0, 0))
    ag_finish(COLS, col_slot(me_mp))

    norm_final, tot, tot_in = ref.norm_final, ref.tot, ref.tot_in
    normalize(COLS, ref.gain_final, norm_final)
    tot[...] = jnp.zeros_like(tot)
    capped_of = []
    for p in range(2):
        raw = nt(table_in[p], norm_final[p * half : (p + 1) * half, :]) / root
        capped = LOGIT_CAP * jnp.tanh(raw / LOGIT_CAP)
        capped_of.append(capped)
        tot[p : p + 1, :] = jnp.sum(jnp.exp(capped), axis=0, keepdims=True)
        tot[2 + p : 3 + p, :] = jnp.sum(jnp.where(hits(p), capped, 0.0), axis=0, keepdims=True)

    def tot_copy(off):
        return pltpu.make_async_remote_copy(
            src_ref=tot,
            dst_ref=tot_in.at[off],
            send_sem=ref.tot_sems.at[0, off],
            recv_sem=ref.tot_sems.at[1, off],
            device_id={"mp": lax.rem(me_mp + off, n_mp)},
            device_id_type=MESH,
        )

    for off in offsets:
        tot_copy(off).start()
    totals = tot[...]
    for off in offsets:
        tot_copy(off).wait_recv()
        totals = totals + tot_in[off]
    ref.nll[...] = jnp.log(totals[0:2, :]) - totals[2:4, :]
    d_logits = []
    for p in range(2):
        capped = capped_of[p]
        ratio = capped / LOGIT_CAP
        d_logit = (
            (jnp.exp(capped) / totals[p : p + 1, :] - hits(p).astype(FL))
            * ref.scale[p : p + 1, :]
            * (1.0 - ratio * ratio)
        ).astype(BF)
        d_logits.append(d_logit)
        part[ROWS, p * half : (p + 1) * half, :] = tn(d_logit, table_in[p]).astype(BF)
    rs_start(ROWS, col_slot)
    for p in range(2):
        ref.table[p] = nn(d_logits[p], norm_final[p * half : (p + 1) * half, :]) / root
    d_final = rs_finish(ROWS, col_slot) / root
    d_out = norm_back(own(COLS, col_slot(me_mp)), d_final, ref.gain_final[...].astype(FL))
    a2a_start(2, d_out, 0, 0)
    ag_start(ROWS, me_mp, a2a_finish(2, 0, 0))
    ag_finish(ROWS, me_mp)

    d_hidden, d_gate_up = ref.d_hidden, ref.d_gate_up
    ff = hidden.shape[1]
    d_hidden[...] = nn(full[ROWS], ref.w_down[...])

    @pl.loop(0, n_mp)
    def _(i):
        where = block(i, size)
        gate, d_hid = gate_pre[where, :], d_hidden[where, :]
        sig = jax.nn.sigmoid(gate)
        d_gate = d_hid * up_proj[where, :] * sig * (1.0 + gate * (1.0 - sig))
        d_gate_up[where, :ff] = d_gate.astype(BF)
        d_gate_up[where, ff:] = (d_hid * gate * sig).astype(BF)

    part[D_MID] = (
        nt(d_gate_up[:, :ff], ref.w_gate[...]) + nt(d_gate_up[:, ff:], ref.w_up[...])
    ).astype(BF)
    rs_start(D_MID, row_slot)
    mlp = Ring(me_dp, ref, MLP)
    attn = Ring(me_dp, ref, ATTN)
    weight_terms(norm_mlp, d_gate_up, mlp.terms, slice(0, 2 * ff))
    weight_terms(full.at[ROWS], hidden, mlp.terms, slice(2 * ff, 3 * ff))
    mlp.pair()
    d_mid = own(ROWS, me_mp) + norm_back(
        own(MID, me_mp), rs_finish(D_MID, row_slot), ref.gain_mlp[...].astype(FL)
    )
    ag_start(D_MID, me_mp, d_mid)
    mlp.step(0)
    ag_finish(D_MID, me_mp)

    d_qkv = ref.d_qkv
    d_attn = nn(full[D_MID], ref.w_out[...]).astype(BF)
    mlp.step(1)
    d_query = jnp.zeros((tokens, head_cols), FL)
    d_key = jnp.zeros((tokens, head_cols), FL)
    d_value = jnp.zeros((tokens, head_cols), FL)
    for h, mask in enumerate(head_masks):
        weights = prob[h]
        d_attn_h = d_attn * mask
        d_prob = nt(d_attn_h, value_rows)
        ratio = score[h] / ATTN_CAP
        d_score = weights * (d_prob - jnp.sum(weights * d_prob, axis=-1, keepdims=True))
        d_scaled = (d_score * (1.0 - ratio * ratio) / math.sqrt(HS)).astype(BF)
        d_query = d_query + nn(d_scaled, key_rows * mask)
        d_key = d_key + tn(d_scaled, queries * mask)
        d_value = d_value + tn(weights.astype(BF), d_attn_h)
    d_qkv[:, :head_cols] = d_query.astype(BF)
    d_qkv[:, head_cols : 2 * head_cols] = d_key.astype(BF)
    d_qkv[:, 2 * head_cols :] = d_value.astype(BF)
    part[D_EMBED] = nt(d_qkv[...], ref.w_qkv[...]).astype(BF)
    rs_start(D_EMBED, row_slot)
    weight_terms(norm_attn, d_qkv, attn.terms, slice(0, 3 * head_cols))
    weight_terms(full.at[D_MID], attn_out, attn.terms, slice(3 * head_cols, 4 * head_cols))
    attn.pair()
    mlp.step(2)
    attn.step(0)
    d_in = own(D_MID, me_mp) + norm_back(
        own(EMBED, me_mp), rs_finish(D_EMBED, row_slot), ref.gain_attn[...].astype(FL)
    )
    a2a_start(3, d_in, 1 - parity, 0)
    mlp.step(3)
    attn.step(1)
    d_embed = a2a_finish(3, 1 - parity, 0)
    keep = jnp.where((me_dp == n_dp - 1) & (parity == 0), 0.0, 1.0)
    ag_start(D_EMBED, other_col_slot(me_mp), d_embed * keep)
    mlp.step(4)
    attn.step(2)
    mlp.step(5)
    attn.step(3)
    ag_finish(D_EMBED, other_col_slot(me_mp))
    for p in range(2):
        ref.table[p] = ref.table[p] + nn(
            hits(p).astype(FL).astype(BF), full[D_EMBED, p * half : (p + 1) * half, :]
        )
    mlp.step(6)
    attn.step(4)
    mlp.cross()
    attn.step(5)
    attn.step(6)
    ref.mlp_sum[...] = mlp.result()
    attn.cross()
    ref.attn_sum[...] = attn.result()

    for stage in range(6):
        sent = part.at[stage, pl.ds(0, (n_mp - 1) * size)]
        for sem in (ref.rs_send, ref.ag_send):
            pltpu.make_async_remote_copy(
                src_ref=sent,
                dst_ref=sent,
                send_sem=sem.at[stage],
                recv_sem=ref.rs_recv.at[stage, 0],
                device_id={"mp": lax.rem(me_mp + 1, n_mp)},
                device_id_type=MESH,
            ).wait_send()
    for which in range(4):
        a2a_all(which).wait_send()
    for off in offsets:
        tot_copy(off).wait_send()
    mlp.drain()
    attn.drain()


def ring_scratch(prefix, n_dp, width, columns):
    dma = pltpu.SemaphoreType.DMA
    length = n_dp // 4
    rows = width // n_dp
    sizes = dict(
        terms=pltpu.VMEM((n_dp, rows, columns), FL),
        pair_out=pltpu.VMEM((length, 2, rows, columns), BF),
        pair_in=pltpu.VMEM((length, 2, rows, columns), BF),
        hop_out=pltpu.VMEM((2, length - 1, 2, rows, columns // 2), BF),
        hop_in=pltpu.VMEM((2, length - 1, 2, rows, columns // 2), BF),
        last=pltpu.VMEM((2, rows, columns), FL),
        y_out=pltpu.VMEM((rows, columns), BF),
        y_in=pltpu.VMEM((rows, columns), BF),
        pair_sems=dma((2, length)),
        hop_send=dma((2, length - 1)),
        hop_recv=dma((2, length - 1)),
        y_sems=dma((2,)),
    )
    return {prefix + name: value for name, value in sizes.items()}


def local(
    token_ids,
    fanout,
    table_of_column,
    embed_table,
    start_vector,
    gain_attn,
    gain_mlp,
    gain_final,
    w_qkv,
    w_out,
    w_gate,
    w_up,
    w_down,
):
    me_mp = lax.axis_index("mp")
    n_mp = lax.axis_size("mp")
    n_dp = lax.axis_size("dp")
    own_cols, vocab_part, width = embed_table.shape
    row_count = token_ids.shape[0]
    rows = row_count // n_dp
    tokens = row_count * own_cols
    head_cols = w_qkv.shape[2]
    heads = head_cols // HS
    ff = w_gate.shape[1]
    size = tokens // n_mp
    parts = width // LANES
    dma = pltpu.SemaphoreType.DMA

    def by_column(values):
        return values.reshape(n_dp, rows, own_cols).transpose(2, 1, 0).reshape(own_cols, row_count)

    ids = by_column(token_ids) - me_mp * vocab_part
    select = table_of_column[None, :, None] == jnp.arange(TABLES, dtype=jnp.int32)[None, None, :]
    counts = jnp.sum(jnp.where(select, fanout[:, None, :], 0), axis=-1).astype(FL)
    scale = by_column(1.0 / (counts * row_count))

    whole = dict(
        ids=ids,
        scale=scale,
        start=start_vector.reshape(1, width),
        gain_attn=gain_attn.reshape(1, width),
        gain_mlp=gain_mlp.reshape(1, width),
        gain_final=gain_final.reshape(1, width),
    )
    stay = dict(
        table_in_hbm=embed_table,
        w_qkv_hbm=w_qkv.reshape(width, 3 * head_cols),
        w_out_hbm=w_out,
        w_gate_hbm=w_gate,
        w_up_hbm=w_up,
        w_down_hbm=w_down,
    )
    outs = dict(
        nll=jax.ShapeDtypeStruct((own_cols, row_count), FL),
        table=jax.ShapeDtypeStruct(embed_table.shape, FL),
        attn_sum=jax.ShapeDtypeStruct((width // n_dp, 4 * head_cols), FL),
        mlp_sum=jax.ShapeDtypeStruct((width // n_dp, 3 * ff), FL),
    )
    scratch = {name.removesuffix(HBM): pltpu.VMEM(array.shape, BF) for name, array in stay.items()}
    scratch |= dict(
        load_sem=dma((len(stay),)),
        part=pltpu.VMEM((6, tokens, width), BF),
        land=pltpu.VMEM((6, n_mp, size, width), BF),
        full=pltpu.VMEM((6, tokens, width), BF),
        rs_send=dma((6,)),
        rs_recv=dma((6, n_mp)),
        ag_send=dma((6,)),
        ag_recv=dma((6, n_mp)),
        wide=pltpu.VMEM((size * parts, LANES), FL),
        outgo=pltpu.VMEM((4, size, parts, LANES), BF),
        income=pltpu.VMEM((4, size, parts, LANES), BF),
        a2a_send=dma((4,)),
        a2a_recv=dma((4,)),
        norm_attn=pltpu.VMEM((tokens, width), BF),
        norm_mlp=pltpu.VMEM((tokens, width), BF),
        norm_final=pltpu.VMEM((tokens, width), BF),
        qkv=pltpu.VMEM((tokens, 3 * head_cols), BF),
        d_qkv=pltpu.VMEM((tokens, 3 * head_cols), BF),
        attn_out=pltpu.VMEM((tokens, head_cols), BF),
        score=pltpu.VMEM((heads, tokens, tokens), FL),
        prob=pltpu.VMEM((heads, tokens, tokens), FL),
        gate_pre=pltpu.VMEM((tokens, ff), FL),
        up_proj=pltpu.VMEM((tokens, ff), FL),
        d_hidden=pltpu.VMEM((tokens, ff), FL),
        hidden=pltpu.VMEM((tokens, ff), BF),
        d_gate_up=pltpu.VMEM((tokens, 2 * ff), BF),
        tot=pltpu.VMEM((8, LANES), FL),
        tot_in=pltpu.VMEM((n_mp, 8, LANES), FL),
        tot_sems=dma((2, n_mp)),
    )
    scratch |= ring_scratch(MLP, n_dp, width, 3 * ff)
    scratch |= ring_scratch(ATTN, n_dp, width, 4 * head_cols)
    vmem = pl.BlockSpec(memory_space=pltpu.VMEM)
    names = (*whole, *stay, *outs, *scratch)
    nll, table_grad, attn_sum, mlp_sum = pl.pallas_call(
        functools.partial(window_kernel, n_dp, n_mp, names),
        out_shape=tuple(outs.values()),
        in_specs=[vmem] * len(whole) + [pl.BlockSpec(memory_space=pl.ANY)] * len(stay),
        out_specs=(vmem,) * len(outs),
        scratch_shapes=list(scratch.values()),
        compiler_params=pltpu.CompilerParams(
            collective_id=1, has_side_effects=True, vmem_limit_bytes=63_000_000
        ),
        name="window",
    )(*whole.values(), *stay.values())
    qkv_width = 3 * head_cols
    return (
        nll.reshape(own_cols, rows, n_dp).transpose(2, 1, 0).reshape(row_count, own_cols),
        table_grad,
        attn_sum[:, :qkv_width].reshape(attn_sum.shape[0], 3, head_cols),
        attn_sum[:, qkv_width:],
        mlp_sum[:, :ff],
        mlp_sum[:, ff : 2 * ff],
        mlp_sum[:, 2 * ff :],
    )


def solution(mesh):
    return jax.shard_map(
        local,
        mesh=mesh,
        in_specs=(
            P(None, "dp"),
            P(),
            P("dp"),
            P("dp", "mp", None),
            P(),
            P(),
            P(),
            P(),
            P(None, None, "mp"),
            P(None, "mp"),
            P(None, "mp"),
            P(None, "mp"),
            P(None, "mp"),
        ),
        out_specs=(
            P(None, "dp"),
            P("dp", "mp", None),
            P("dp", None, "mp"),
            P("dp", "mp"),
            P("dp", "mp"),
            P("dp", "mp"),
            P("dp", "mp"),
        ),
        check_vma=False,
    )
```

time: 728 us -> 183 us (0.25)
  waiting for transfers between devices: 364 us -> 0 us
  blocking collectives: 230 us -> 0 us
  Pallas kernels: 0 us -> 164 us
  matrix products: 46 us -> 0 us
  starting transfers between devices: 30.4 us -> 0 us
  other arithmetic: 18.3 us -> 0.86 us
  between operations: 14.7 us -> 0.71 us
  local copies, waits for them, and re-layouts: 22.4 us -> 14.8 us
    reduce_scatter x5 -> x0, waiting for transfers between devices: 170 us -> none  [feature_sum(): return lax.psum_scatter(term, 'mp', scatter_dimension=2, tiled=True)]
    pallas_call x0 -> x1, Pallas kernels: none -> 164 us  [local(): pl.pallas_call(functools.partial(window_kernel, n_dp, n_mp, names), out_s...]
    all_gather x6 -> x0, blocking collectives: 161 us -> none  [gather_features(): return lax.all_gather(values, 'mp', axis=2, tiled=True)]
    unnamed x8 -> x0, waiting for transfers between devices: 90.5 us -> none
    psum x1 -> x0, waiting for transfers between devices: 76.1 us -> none  [local(): d_final = lax.psum(d_final_part, 'mp')]
    psum x3 -> x0, blocking collectives: 49.6 us -> none  [the longest x2 31.7 us: local(): lax.psum((jnp.sum(exp_logit, axis=-1), jnp.sum(capped * onehot_f, axis=-1...]
    dot_general x26 -> x0, matrix products: 46 us -> none  [the longest x1 2.85 us: local(): jnp.einsum('rpd,rpf->df', norm_mlp, d_gate, preferred_element_type=fl)]
    all_to_all x3 -> x0, starting transfers between devices: 30 us -> none  [the longest x2 20 us: rows_to_cols(): return lax.all_to_all(values, 'dp', split_axis=1, concat_axis=0, tiled=True)]
  transfers between devices with their start and end apart: 10 -> 0, of which waited for: 10 -> 0; matrix products, arithmetic and copies ran while one was open for 5% -> 0% of each run, Pallas kernels for 0% -> 0%
where the time goes in v2:
time: 183 us; the launch traced here: 180 us
  Pallas kernels  164 us (90%)
  local copies, waits for them, and re-layouts  14.8 us (8%)
    pallas_call x1, Pallas kernels, local(): pl.pallas_call(functools.partial(window_kernel, n_dp, n_mp, names), out_s...  164 us
    unnamed x17, local copies, waits for them, and re-layouts  6.08 us

profile of v2, /device:TPU:2, one launch (start us, length us, event | category | flops | bytes accessed | tf_op | source)
XLA Modules:
  0.0 180.5 jit_solution(4357989263796162515)
XLA Ops:
  0.7 0.7 broadcast_subtract_fusion
  1.4 0.1 select_reduce_fusion
  1.5 0.7 copy-done.2
  2.2 0.6 reshape.78.refs_2_
  2.8 0.1 copy-done.3
  2.9 0.6 reshape.79.refs_3_
  3.5 0.1 copy-done.4
  3.6 0.6 reshape.80.refs_4_
  4.2 0.1 copy-done.5
  4.3 0.6 reshape.81.refs_5_
  4.9 0.1 div.12
  5.0 0.7 reshape.77.refs_1_
  5.7 0.1 sub.14
  5.9 0.7 sub.16.refs_0_
  6.5 1.4 copy.34
  8.0 1.2 copy.35.refs_7_
  9.1 164.1 %window.1 = (f32[2,128]{1,0:T(2,128)}, f32[2,128,1024]{2,1,0:T(8,128)}, f32[32,512]{1,0:T(8,128)}, f32[32,1536]{1,0:T(8,128)}) custom-call(s32[2,128]{1,0:T(2,128)} %sub.16.refs_0_, f32[2,128]{1,0:T(2,128)} %reshape.77.refs_1_, bf16[1,1024]{1,0:T(2,128)(2,1)} %reshape.78.refs_2_, bf16[1,1024]{1,0:T(2,128)(2,1)} %reshape.79.refs_3_, ...), custom_call_target="tpu_custom_call" | custom-call | tf_op jit(solution)/shard_map/window/pallas_call | solution.py:641
  173.2 0.8 reshape.83
  174.0 1.3 slice.16
  175.3 1.4 copy_bitcast_fusion
  176.7 0.1 copy.36
  176.8 0.7 reshape.84
  177.5 0.7 fusion
  178.2 2.3 %copy.41 = f32[2,128,1024]{2,1,0:T(8,128)} copy(f32[2,128,1024]{2,1,0:T(8,128)} %get-tuple-element.47) | data formatting | bytes 2097152
  (14 shorter events, 0.3 us)
Async XLA Ops:
  0.6 0.8 copy-start.1
  0.6 0.7 copy-start.6
  1.5 0.7 copy-start.2
  2.2 0.7 copy-start.3
  2.9 0.7 copy-start.4
  3.6 0.7 copy-start.5
  173.2 4.3 %copy-start = (f32[32,1536]{1,0:T(8,128)S(1)}, f32[32,1536]{1,0:T(8,128)}, u32[]{:S(2)}) copy-start(f32[32,1536]{1,0:T(8,128)} %get-tuple-element.14) | copy-start | bytes 589828

commit v3 on v2

--- a/solution.py
+++ b/solution.py
@@ -163,9 +163,22 @@
     loads = types.SimpleNamespace()
     for slot, name in enumerate(name for name in names if name.endswith(HBM)):
         here = name.removesuffix(HBM)
+        if here == "w_qkv":
+            continue
         copy = pltpu.make_async_copy(getattr(ref, name), getattr(ref, here), ref.load_sem.at[slot])
         copy.start()
         setattr(loads, here, copy)
+    head_width = ref.attn_out.shape[1]
+    qkv_loads = [
+        pltpu.make_async_copy(
+            ref.w_qkv_hbm.at[t],
+            ref.w_qkv.at[:, t * head_width : (t + 1) * head_width],
+            ref.qkv_sem.at[t],
+        )
+        for t in range(3)
+    ]
+    for copy in qkv_loads:
+        copy.start()
 
     barrier = pltpu.get_barrier_semaphore()
     for axis, me, count in (("mp", me_mp, n_mp), ("dp", me_dp, n_dp)):
@@ -211,25 +224,52 @@
             total = total + land[stage, off].astype(FL)
         return total
 
-    def ag_copy(stage, off, slot):
-        where = full.at[stage, block(slot, size)]
+    ring = n_mp // 2
+    m_x, m_y = me_mp // 2, lax.rem(me_mp, 2)
+
+    def place(dx, dy):
+        return 2 * lax.rem(m_x + dx, ring) + (1 - m_y if dy else m_y)
+
+    def ag_copy(stage, channel, origin, peer, slot_of, rows=(0, 2)):
+        start, stop = rows
+        piece = size // 2
+        first_row = pl.multiple_of(slot_of(origin) * size + start * piece, piece)
+        where = full.at[stage, pl.ds(first_row, (stop - start) * piece)]
         return pltpu.make_async_remote_copy(
             src_ref=where,
             dst_ref=where,
             send_sem=ref.ag_send.at[stage],
-            recv_sem=ref.ag_recv.at[stage, off],
-            device_id={"mp": lax.rem(me_mp + off, n_mp)},
+            recv_sem=ref.ag_recv.at[stage, channel],
+            device_id={"mp": peer},
             device_id_type=MESH,
         )
 
-    def ag_start(stage, slot, values):
-        full[stage, block(slot, size), :] = values.astype(BF)
-        for off in offsets:
-            ag_copy(stage, off, slot).start()
-
-    def ag_finish(stage, slot):
-        for off in offsets:
-            ag_copy(stage, off, slot).wait_recv()
+    up, down, far = 1, ring - 1, ring // 2
+
+    def ag_start(stage, slot_of, values):
+        full[stage, block(slot_of(me_mp), size), :] = values.astype(BF)
+        ag_copy(stage, 0, me_mp, place(0, 1), slot_of).start()
+        ag_copy(stage, 1, me_mp, place(up, 0), slot_of).start()
+        ag_copy(stage, 2, me_mp, place(down, 0), slot_of).start()
+
+    def ag_got(stage, channel, origin, slot_of, rows=(0, 2)):
+        ag_copy(stage, channel, origin, place(0, 1), slot_of, rows).wait_recv()
+
+    def ag_finish(stage, slot_of):
+        twin = place(0, 1)
+        ag_got(stage, 0, twin, slot_of)
+        ag_copy(stage, 3, twin, place(up, 0), slot_of).start()
+        ag_copy(stage, 4, twin, place(down, 0), slot_of).start()
+        ag_got(stage, 1, place(down, 0), slot_of)
+        ag_copy(stage, 5, place(down, 0), place(up, 0), slot_of, (0, 1)).start()
+        ag_got(stage, 2, place(up, 0), slot_of)
+        ag_copy(stage, 6, place(up, 0), place(down, 0), slot_of, (1, 2)).start()
+        ag_got(stage, 5, place(far, 0), slot_of, (0, 1))
+        ag_got(stage, 6, place(far, 0), slot_of, (1, 2))
+        ag_copy(stage, 7, place(far, 0), twin, slot_of).start()
+        ag_got(stage, 3, place(down, 1), slot_of)
+        ag_got(stage, 4, place(up, 1), slot_of)
+        ag_got(stage, 7, place(far, 1), slot_of)
 
     wide, outgo, income = ref.wide, ref.outgo, ref.income
 
@@ -282,7 +322,7 @@
         @pl.loop(0, n_mp)
         def _(i):
             floats = full[stage, block(i, size), :].astype(FL)
-            out[block(i, size), :] = (floats / rms_of(floats) * gain[...].astype(FL)).astype(BF)
+            out[block(i, size), :] = (floats / rms_of(floats) * ref.vectors[gain : gain + 1, :]).astype(BF)
 
     def weight_terms(left, right, out, cols):
         @pl.loop(0, width // LANES)
@@ -305,14 +345,15 @@
     a2a_start(0, rs_finish(EMBED, other_col_slot), 0, 1 - parity)
     values = a2a_finish(0, 0, 1 - parity)
     first = lax.broadcasted_iota(jnp.int32, values.shape, 0) + parity == 0
-    values = jnp.where(first, ref.start[...].astype(FL), values)
-    ag_start(EMBED, me_mp, values)
-    ag_finish(EMBED, me_mp)
+    values = jnp.where(first, ref.vectors[0:1, :], values)
+    ag_start(EMBED, row_slot, values)
+    ag_finish(EMBED, row_slot)
 
     norm_attn, qkv, attn_out = ref.norm_attn, ref.qkv, ref.attn_out
     score, prob = ref.score, ref.prob
-    normalize(EMBED, ref.gain_attn, norm_attn)
-    loads.w_qkv.wait()
+    normalize(EMBED, 1, norm_attn)
+    for copy in qkv_loads:
+        copy.wait()
     qkv[...] = nn(norm_attn[...], ref.w_qkv[...]).astype(BF)
     head_cols = attn_out.shape[1]
     lane = lax.broadcasted_iota(jnp.int32, (1, head_cols), 1)
@@ -345,8 +386,8 @@
     loads.w_out.wait()
     part[MID] = nt(attn_out[...], ref.w_out[...]).astype(BF)
     rs_start(MID, row_slot)
-    ag_start(MID, me_mp, own(EMBED, me_mp) + rs_finish(MID, row_slot))
-    ag_finish(MID, me_mp)
+    ag_start(MID, row_slot, own(EMBED, me_mp) + rs_finish(MID, row_slot))
+    ag_finish(MID, row_slot)
 
     norm_mlp, gate_pre, up_proj, hidden = (
         ref.norm_mlp,
@@ -354,7 +395,7 @@
         ref.up_proj,
         ref.hidden,
     )
-    normalize(MID, ref.gain_mlp, norm_mlp)
+    normalize(MID, 2, norm_mlp)
     loads.w_gate.wait()
     gate_pre[...] = nn(norm_mlp[...], ref.w_gate[...])
     loads.w_up.wait()
@@ -370,11 +411,11 @@
     part[COLS] = nt(hidden[...], ref.w_down[...]).astype(BF)
     rs_start(COLS, row_slot)
     a2a_start(1, own(MID, me_mp) + rs_finish(COLS, row_slot), 0, 0)
-    ag_start(COLS, col_slot(me_mp), a2a_finish(1, 0, 0))
-    ag_finish(COLS, col_slot(me_mp))
+    ag_start(COLS, col_slot, a2a_finish(1, 0, 0))
+    ag_finish(COLS, col_slot)
 
     norm_final, tot, tot_in = ref.norm_final, ref.tot, ref.tot_in
-    normalize(COLS, ref.gain_final, norm_final)
+    normalize(COLS, 3, norm_final)
     tot[...] = jnp.zeros_like(tot)
     capped_of = []
     for p in range(2):
@@ -416,10 +457,10 @@
     for p in range(2):
         ref.table[p] = nn(d_logits[p], norm_final[p * half : (p + 1) * half, :]) / root
     d_final = rs_finish(ROWS, col_slot) / root
-    d_out = norm_back(own(COLS, col_slot(me_mp)), d_final, ref.gain_final[...].astype(FL))
+    d_out = norm_back(own(COLS, col_slot(me_mp)), d_final, ref.vectors[3:4, :])
     a2a_start(2, d_out, 0, 0)
-    ag_start(ROWS, me_mp, a2a_finish(2, 0, 0))
-    ag_finish(ROWS, me_mp)
+    ag_start(ROWS, row_slot, a2a_finish(2, 0, 0))
+    ag_finish(ROWS, row_slot)
 
     d_hidden, d_gate_up = ref.d_hidden, ref.d_gate_up
     ff = hidden.shape[1]
@@ -444,11 +485,11 @@
     weight_terms(full.at[ROWS], hidden, mlp.terms, slice(2 * ff, 3 * ff))
     mlp.pair()
     d_mid = own(ROWS, me_mp) + norm_back(
-        own(MID, me_mp), rs_finish(D_MID, row_slot), ref.gain_mlp[...].astype(FL)
-    )
-    ag_start(D_MID, me_mp, d_mid)
+        own(MID, me_mp), rs_finish(D_MID, row_slot), ref.vectors[2:3, :]
+    )
+    ag_start(D_MID, row_slot, d_mid)
     mlp.step(0)
-    ag_finish(D_MID, me_mp)
+    ag_finish(D_MID, row_slot)
 
     d_qkv = ref.d_qkv
     d_attn = nn(full[D_MID], ref.w_out[...]).astype(BF)
@@ -477,19 +518,19 @@
     mlp.step(2)
     attn.step(0)
     d_in = own(D_MID, me_mp) + norm_back(
-        own(EMBED, me_mp), rs_finish(D_EMBED, row_slot), ref.gain_attn[...].astype(FL)
+        own(EMBED, me_mp), rs_finish(D_EMBED, row_slot), ref.vectors[1:2, :]
     )
     a2a_start(3, d_in, 1 - parity, 0)
     mlp.step(3)
     attn.step(1)
     d_embed = a2a_finish(3, 1 - parity, 0)
     keep = jnp.where((me_dp == n_dp - 1) & (parity == 0), 0.0, 1.0)
-    ag_start(D_EMBED, other_col_slot(me_mp), d_embed * keep)
+    ag_start(D_EMBED, other_col_slot, d_embed * keep)
     mlp.step(4)
     attn.step(2)
     mlp.step(5)
     attn.step(3)
-    ag_finish(D_EMBED, other_col_slot(me_mp))
+    ag_finish(D_EMBED, other_col_slot)
     for p in range(2):
         ref.table[p] = ref.table[p] + nn(
             hits(p).astype(FL).astype(BF), full[D_EMBED, p * half : (p + 1) * half, :]
@@ -499,9 +540,14 @@
     mlp.cross()
     attn.step(5)
     attn.step(6)
-    ref.mlp_sum[...] = mlp.result()
+    mlp_sum = mlp.result()
+    for i, out in enumerate((ref.sum_gate, ref.sum_up, ref.sum_down)):
+        out[...] = mlp_sum[:, i * ff : (i + 1) * ff]
     attn.cross()
-    ref.attn_sum[...] = attn.result()
+    attn_sum = attn.result()
+    for t in range(3):
+        ref.sum_qkv[t] = attn_sum[:, t * head_cols : (t + 1) * head_cols]
+    ref.sum_out[...] = attn_sum[:, 3 * head_cols :]
 
     for stage in range(6):
         sent = part.at[stage, pl.ds(0, (n_mp - 1) * size)]
@@ -583,14 +629,11 @@
     whole = dict(
         ids=ids,
         scale=scale,
-        start=start_vector.reshape(1, width),
-        gain_attn=gain_attn.reshape(1, width),
-        gain_mlp=gain_mlp.reshape(1, width),
-        gain_final=gain_final.reshape(1, width),
+        vectors=jnp.stack([start_vector, gain_attn, gain_mlp, gain_final]).astype(FL),
     )
     stay = dict(
         table_in_hbm=embed_table,
-        w_qkv_hbm=w_qkv.reshape(width, 3 * head_cols),
+        w_qkv_hbm=w_qkv.transpose(1, 0, 2),
         w_out_hbm=w_out,
         w_gate_hbm=w_gate,
         w_up_hbm=w_up,
@@ -599,11 +642,16 @@
     outs = dict(
         nll=jax.ShapeDtypeStruct((own_cols, row_count), FL),
         table=jax.ShapeDtypeStruct(embed_table.shape, FL),
-        attn_sum=jax.ShapeDtypeStruct((width // n_dp, 4 * head_cols), FL),
-        mlp_sum=jax.ShapeDtypeStruct((width // n_dp, 3 * ff), FL),
+        sum_qkv=jax.ShapeDtypeStruct((3, width // n_dp, head_cols), FL),
+        sum_out=jax.ShapeDtypeStruct((width // n_dp, head_cols), FL),
+        sum_gate=jax.ShapeDtypeStruct((width // n_dp, ff), FL),
+        sum_up=jax.ShapeDtypeStruct((width // n_dp, ff), FL),
+        sum_down=jax.ShapeDtypeStruct((width // n_dp, ff), FL),
     )
     scratch = {name.removesuffix(HBM): pltpu.VMEM(array.shape, BF) for name, array in stay.items()}
     scratch |= dict(
+        w_qkv=pltpu.VMEM((width, 3 * head_cols), BF),
+        qkv_sem=dma((3,)),
         load_sem=dma((len(stay),)),
         part=pltpu.VMEM((6, tokens, width), BF),
         land=pltpu.VMEM((6, n_mp, size, width), BF),
@@ -638,7 +686,7 @@
     scratch |= ring_scratch(ATTN, n_dp, width, 4 * head_cols)
     vmem = pl.BlockSpec(memory_space=pltpu.VMEM)
     names = (*whole, *stay, *outs, *scratch)
-    nll, table_grad, attn_sum, mlp_sum = pl.pallas_call(
+    nll, table_grad, sum_qkv, *sums = pl.pallas_call(
         functools.partial(window_kernel, n_dp, n_mp, names),
         out_shape=tuple(outs.values()),
         in_specs=[vmem] * len(whole) + [pl.BlockSpec(memory_space=pl.ANY)] * len(stay),
@@ -649,15 +697,11 @@
         ),
         name="window",
     )(*whole.values(), *stay.values())
-    qkv_width = 3 * head_cols
     return (
         nll.reshape(own_cols, rows, n_dp).transpose(2, 1, 0).reshape(row_count, own_cols),
         table_grad,
-        attn_sum[:, :qkv_width].reshape(attn_sum.shape[0], 3, head_cols),
-        attn_sum[:, qkv_width:],
-        mlp_sum[:, :ff],
-        mlp_sum[:, ff : 2 * ff],
-        mlp_sum[:, 2 * ff :],
+        sum_qkv.transpose(1, 0, 2),
+        *sums,
     )
 
 

time: 183 us -> 194 us (1.060)
  Pallas kernels: 164 us -> 178 us
    pallas_call x1, Pallas kernels: 164 us -> 178 us  [local(): pl.pallas_call(functools.partial(window_kernel, n_dp, n_mp, names), out_s...]
    unnamed x17 -> x32, local copies, waits for them, and re-layouts: 6.08 us -> 10.7 us
    reshape x5 -> x0, local copies, waits for them, and re-layouts: 3.54 us -> none  [the longest x1 1.15 us: local(): w_qkv.reshape(width, 3 * head_cols)]
    slice x2 -> x0, local copies, waits for them, and re-layouts: 2 us -> none  [the longest x1 1.32 us: local(): attn_sum[:, qkv_width:]]
where the time goes in v3:
time: 194 us; the launch traced here: 192 us
  Pallas kernels  178 us (92%)
  local copies, waits for them, and re-layouts  13.2 us (7%)
    pallas_call x1, Pallas kernels, local(): pl.pallas_call(functools.partial(window_kernel, n_dp, n_mp, names), out_s...  178 us
    unnamed x32, local copies, waits for them, and re-layouts  10.7 us

profile of v3, /device:TPU:2, one launch (start us, length us, event | category | flops | bytes accessed | tf_op | source)
XLA Modules:
  0.0 192.4 jit_solution(5315249926076049426)
XLA Ops:
  0.7 0.7 copy-done.11
  1.3 0.7 copy-done.12
  2.2 0.7 copy-done.6
  2.8 0.7 copy-done.7
  3.5 0.7 copy-done.8
  4.2 0.7 copy-done.9
  4.9 0.6 maximum_convert_fusion.refs_2_
  5.5 0.1 div.12
  5.7 0.7 reshape.59.refs_1_
  6.4 0.1 sub.14
  6.5 0.7 sub.16.refs_0_
  7.2 177.7 %window.1 = (f32[2,128]{1,0:T(2,128)}, f32[2,128,1024]{2,1,0:T(8,128)}, f32[3,32,128]{2,1,0:T(8,128)}, f32[32,128]{1,0:T(8,128)}, f32[32,512]{1,0:T(8,128)}, /*index=5*/f32[32,512]{1,0:T(8,128)}, f32[32,512]{1,0:T(8,128)}) custom-call(s32[2,128]{1,0:T(2,128)} %sub.16.refs_0_, f32[2,128]{1,0:T(2,128)} %reshape.59.refs_1_, ...), custom_call_target="tpu_custom_call" | custom-call | tf_op jit(solution)/shard_map/window/pallas_call | solution.py:689
  184.9 0.7 copy-done.10
  185.7 0.1 copy.29
  185.7 0.7 reshape.61
  186.4 2.3 %copy.36 = f32[2,128,1024]{2,1,0:T(8,128)} copy(f32[2,128,1024]{2,1,0:T(8,128)} %get-tuple-element.29) | data formatting | bytes 2097152
  188.7 0.6 copy.37
  189.4 0.1 copy-done.4
  189.5 0.6 copy.38
  190.1 0.6 copy.39
  190.7 0.2 copy-done.1
  190.9 0.6 copy.40
  191.6 0.2 copy-done
  191.8 0.6 copy.41
  (27 shorter events, 0.5 us)
Async XLA Ops:
  0.6 1.4 copy-start.5
  0.6 0.7 copy-start.11
  1.3 0.7 copy-start.12
  2.2 0.7 copy-start.6
  2.8 0.7 copy-start.7
  3.5 0.7 copy-start.8
  4.2 0.7 copy-start.9
  184.9 0.7 copy-start.10
  186.4 2.3 %copy-start.3 = (f32[3,32,128]{2,1,0:T(8,128)S(1)}, f32[3,32,128]{2,1,0:T(8,128)}, u32[]{:S(2)}) copy-start(f32[3,32,128]{2,1,0:T(8,128)} %get-tuple-element.16) | copy-start | bytes 147460
  188.7 0.7 copy-start.4
  188.7 1.3 copy-start.2
  190.1 0.9 copy-start.1
  190.9 0.9 copy-start
